TPU v7x, 512 devices: a whole 4x4x16 slice. The times are simulated.
512 devices in a mesh: expert: 8 (over z_hi, x), shard: 64 (over y, z_lo, core).
Axes of the slice: x: 4, y: 4, z: 16 (z_hi: 2, z_lo: 8; z = z_hi * 8 + z_lo), core: 2. Of those that a mesh axis runs over, the one named last changes fastest.
Arguments:
- tokens: bfloat16 [1024, 2048], P('expert', 'shard'), may hold values from -6 to 6
- cotangent: bfloat16 [1024, 2048], P('expert', 'shard'), may hold values from -6 to 6
- expert_ids: int32 [1024, 2], P('expert'), may hold values from 0 to 7, all different within a row; in each aligned block of 128 rows (0 to 127, 128 to 255, ...) at most 48 rows name the same one
- route_weights: float32 [1024, 2], P('expert'), may hold values from 0.2 to 1
- dense_gate: bfloat16 [2048, 11008], P('expert', 'shard'), may hold values from -0.125 to 0.125
- dense_up: bfloat16 [2048, 11008], P('expert', 'shard'), may hold values from -0.125 to 0.125
- dense_down: bfloat16 [11008, 2048], P('shard', 'expert'), may hold values from -0.15625 to 0.15625
- noise_gate: bfloat16 [8, 2048, 1280], P('expert', None, 'shard'), may hold values from -0.125 to 0.125
- noise_up: bfloat16 [8, 2048, 1280], P('expert', None, 'shard'), may hold values from -0.125 to 0.125
- noise_down: bfloat16 [8, 1280, 2048], P('expert', 'shard'), may hold values from -0.0546875 to 0.0546875
Outputs:
- mixed: bfloat16 [1024, 2048], P('expert', 'shard')
- grad_gate: bfloat16 [8, 12288, 2048], P('expert', 'shard')
- grad_up: bfloat16 [8, 12288, 2048], P('expert', 'shard')
- grad_down: bfloat16 [8, 12288, 2048], P('expert', 'shard')
Inputs may be any that keep to these rules, and one draw needn't show every extreme that they name: `expert_ids`: the two experts of a token differ. Within each aligned block of 128 tokens no expert is named by more than 48 tokens, a bound that some block reaches.
All inputs are finite; a program needn't handle non-finite values.
Results may differ from a plain program's by a relative error of at most 0.0058.
Values may be sent and summed in bfloat16 or wider, within the bound.
No kernel may reach another device: no remote copies, remote signals or barrier semaphores. Data moves between devices by JAX's collectives and lax.ppermute only.
A program may use at most 64 MiB of HBM per device.

v0:
```python
import jax
import jax.numpy as jnp
from jax import lax
from jax.sharding import PartitionSpec as P


def local(
    tokens,
    cotangent,
    expert_ids,
    route_weights,
    dense_gate,
    dense_up,
    dense_down,
    noise_gate,
    noise_up,
    noise_down,
):
    experts = lax.axis_size("expert")
    tok_dev = tokens.shape[0]
    capacity = min(tok_dev, 3 * tok_dev // experts)
    rows_total = experts * capacity
    gate_full, up_full = (
        lax.all_gather(dense_gate, "expert", axis=0, tiled=True),
        lax.all_gather(dense_up, "expert", axis=0, tiled=True),
    )
    down_full = lax.all_gather(dense_down, "expert", axis=1, tiled=True)
    wide_gate = jnp.concatenate([gate_full, noise_gate[0]], axis=1)
    wide_up = jnp.concatenate([up_full, noise_up[0]], axis=1)
    wide_down = jnp.concatenate([down_full, noise_down[0]], axis=0)
    pair_ids = expert_ids.reshape(-1)
    onehot = (pair_ids[:, None] == jnp.arange(experts, dtype=jnp.int32)[None, :]).astype(jnp.int32)
    earlier = jnp.cumsum(onehot, axis=0) - onehot
    slot_index = jnp.sum(earlier * onehot, axis=1)
    target = pair_ids * capacity + slot_index
    flat_weights = route_weights.reshape(-1)
    row_width = tokens.shape[1]
    tok_pairs = jnp.repeat(tokens, 2, axis=0)
    cot_pairs = (
        flat_weights[:, None] * jnp.repeat(cotangent, 2, axis=0).astype(jnp.float32)
    ).astype(jnp.bfloat16)
    send_tok = jnp.zeros((rows_total, row_width), jnp.bfloat16).at[target].set(tok_pairs)
    send_cot = jnp.zeros((rows_total, row_width), jnp.bfloat16).at[target].set(cot_pairs)
    send_tok, send_cot = (send_tok, send_cot)
    slot_tok, slot_cot = (
        lax.all_to_all(send_tok, "expert", split_axis=0, concat_axis=0, tiled=True),
        lax.all_to_all(send_cot, "expert", split_axis=0, concat_axis=0, tiled=True),
    )
    inputs, slot_grads = (
        lax.all_gather(slot_tok, "shard", axis=1, tiled=True),
        lax.all_gather(slot_cot, "shard", axis=1, tiled=True),
    )
    gate_pre = jnp.dot(inputs, wide_gate, preferred_element_type=jnp.float32)
    up_pre = jnp.dot(inputs, wide_up, preferred_element_type=jnp.float32)
    sigmoid_gate = jax.nn.sigmoid(gate_pre)
    silu_gate = gate_pre * sigmoid_gate
    hidden = (silu_gate * up_pre).astype(jnp.bfloat16)
    summed = lax.psum_scatter(
        lax.dot_general(
            wide_down, hidden, (((0,), (1,)), ((), ())), preferred_element_type=jnp.float32
        ),
        "shard",
        scatter_dimension=0,
        tiled=True,
    )
    out_slots = summed.astype(jnp.bfloat16)
    returned = lax.all_to_all(out_slots, "expert", split_axis=1, concat_axis=1, tiled=True)
    picked = jnp.take(returned, target, axis=1).astype(jnp.float32)
    weighted = (picked * flat_weights[None, :]).reshape(picked.shape[0], tok_dev, 2)
    mixed = jnp.sum(weighted, axis=2).T.astype(jnp.bfloat16)
    grad_hidden = lax.dot_general(
        slot_grads, wide_down, (((1,), (1,)), ((), ())), preferred_element_type=jnp.float32
    )
    grad_gate_pre = (
        grad_hidden * up_pre * sigmoid_gate * (1.0 + gate_pre * (1.0 - sigmoid_gate))
    ).astype(jnp.bfloat16)
    grad_up_pre = (grad_hidden * silu_gate).astype(jnp.bfloat16)
    contract_rows = (((0,), (0,)), ((), ()))
    grad_gate = lax.dot_general(
        grad_gate_pre, inputs, contract_rows, preferred_element_type=jnp.float32
    ).astype(jnp.bfloat16)
    grad_up = lax.dot_general(
        grad_up_pre, inputs, contract_rows, preferred_element_type=jnp.float32
    ).astype(jnp.bfloat16)
    grad_down = lax.dot_general(
        hidden, slot_grads, contract_rows, preferred_element_type=jnp.float32
    ).astype(jnp.bfloat16)
    return (mixed, grad_gate[None], grad_up[None], grad_down[None])


def solution(mesh):
    in_specs = (
        P("expert", "shard"),
        P("expert", "shard"),
        P("expert", None),
        P("expert", None),
        P("expert", "shard"),
        P("expert", "shard"),
        P("shard", "expert"),
        P("expert", None, "shard"),
        P("expert", None, "shard"),
        P("expert", "shard", None),
    )
    out_specs = (
        P("expert", "shard"),
        P("expert", "shard", None),
        P("expert", "shard", None),
        P("expert", "shard", None),
    )
    return jax.shard_map(local, mesh=mesh, in_specs=in_specs, out_specs=out_specs, check_vma=False)
```

profile of v0, /device:TPU:2, one launch (start us, length us, event | category | flops | bytes accessed | tf_op | source)
XLA Modules:
  0.0 763.7 jit_solution(14176948831567929491)
XLA Ops:
  7.2 0.0 copy-start.4
  7.2 0.0 all-gather.3.cloned.1.call-start
  7.2 0.7 broadcast_multiply_fusion
  7.9 0.8 copy.65
  8.7 0.1 eq.26
  8.8 0.1 reshape.88
  9.0 0.0 copy-start.5
  9.0 0.1 copy.69
  9.1 0.1 mul.65
  9.2 0.6 reduce-window.6
  9.8 0.2 slice_reduce_fusion
  10.1 0.8 copy.70
  10.9 0.1 fusion.22
  11.1 1.2 scatter_custom_fusion
  12.3 0.1 copy.72
  12.4 0.1 reshape.120
  12.5 31.4 %all_to_all.36 = bf16[8,2,768]{2,1,0:T(2,128)(2,1)S(1)} all-to-all(bf16[8,2,768]{2,1,0:T(2,128)(2,1)S(1)} %reshape.120), channel_id=1, replica_groups=mesh['expert'=8,'shard'=64] {'expert'}, dimensions={0} | all-to-all | bytes 49152 | tf_op jit(solution)/shard_map/all_to_all | solution.py:46
  43.9 0.1 reshape.121
  44.0 0.0 copy-start.6
  44.1 0.7 all_to_all.26
  44.8 0.0 all-gather.3.cloned.1.call-update
  44.8 0.0 all-gather.5.cloned.1.call-start
  44.8 0.8 copy.76
  45.6 0.8 copy.78
  46.4 0.1 mul.70
  46.6 1.3 scatter_custom_fusion.1
  47.9 0.1 copy.80
  48.0 0.1 reshape.124
  48.2 17.3 %all_to_all.37 = bf16[8,2,768]{2,1,0:T(2,128)(2,1)S(1)} all-to-all(bf16[8,2,768]{2,1,0:T(2,128)(2,1)S(1)} %reshape.124), channel_id=1, replica_groups=mesh['expert'=8,'shard'=64] {'expert'}, dimensions={0} | all-to-all | bytes 49152 | tf_op jit(solution)/shard_map/all_to_all | solution.py:47
  65.5 0.1 reshape.125
  65.6 0.7 all_to_all.32
  66.4 0.0 all-gather.5.cloned.1.call-update
  66.4 0.0 reduce-scatter.2.cloned.1.call-start
  66.4 0.0 copy-done.4
  66.4 56.7 %all_gather.17 = bf16[2048,172]{0,1:T(8,128)(2,1)} all-gather(bf16[256,172]{0,1:T(8,128)(2,1)S(1)} %copy-done.4), channel_id=1, replica_groups=mesh['expert'=8,'shard'=64] {'expert'}, dimensions={0}, use_global_device_ids=true | all-gather | bytes 792576 | tf_op jit(solution)/shard_map/all_gather | solution.py:24
  123.2 67.1 %all_gather.18 = bf16[2048,172]{0,1:T(8,128)(2,1)S(1)} all-gather(bf16[256,172]{0,1:T(8,128)(2,1)S(1)} %copy-done.5), channel_id=1, replica_groups=mesh['expert'=8,'shard'=64] {'expert'}, dimensions={0}, use_global_device_ids=true | all-gather | bytes 792576 | tf_op jit(solution)/shard_map/all_gather | solution.py:25
  190.3 74.2 %all_gather.15 = bf16[172,2048]{1,0:T(8,128)(2,1)S(1)} all-gather(bf16[172,256]{1,0:T(8,128)(2,1)S(1)} %copy-done.6), channel_id=1, replica_groups=mesh['expert'=8,'shard'=64] {'expert'}, dimensions={1}, use_global_device_ids=true | all-gather | bytes 792576 | tf_op jit(solution)/shard_map/all_gather | solution.py:27
  264.5 2.4 fusion.3
  266.9 0.0 copy-start.3
  266.9 1.3 multiply_convert_fusion.2
  268.2 3.3 fusion.12
  271.6 0.0 reduce-scatter.2.cloned.1.call-update
  271.6 0.1 reduce_sum.23
  271.7 0.1 copy.67
  271.8 0.5 copy-done.7
  272.3 0.1 copy.68
  272.4 11.0 %all-gather.5.cloned.1.call-done = bf16[384,2048]{0,1:T(8,128)(2,1)} async-done(((bf16[384,32]{0,1:T(8,128)(2,1)}), bf16[384,2048]{0,1:T(8,128)(2,1)}) %all-gather.5.cloned.1.call-update) | async-done | bytes 1572880 | tf_op jit(solution)/shard_map/all_gather | solution.py:51
  283.5 2.0 fusion.11
  285.4 0.0 copy-start.2
  285.4 1.6 fusion.1
  287.1 0.0 copy-done.2
  287.1 1.6 fusion
  288.7 442.6 %reduce-scatter.2.cloned.1.call-done = f32[32,384]{1,0:T(8,128)} async-done(((f32[2048,384]{1,0:T(8,128)}), f32[32,384]{1,0:T(8,128)}) %reduce-scatter.2.cloned.1.call-update) | async-done | bytes 49168 | tf_op jit(solution)/shard_map/reduce_scatter | solution.py:58
  731.2 0.8 convert_element_type.51
  732.0 0.1 all_to_all.27
  732.2 0.7 reshape.122
  732.9 8.6 %all-to-all-start.1 = ((bf16[8,2,768]{2,1,0:T(2,128)(2,1)}), bf16[8,2,768]{2,1,0:T(2,128)(2,1)S(1)}, u32[]{:S(2)}, u32[]{:S(2)}) async-start(bf16[8,2,768]{2,1,0:T(2,128)(2,1)} %reshape.122), calls=%async_computation.2 | async-start | bytes 49152 | tf_op jit(solution)/shard_map/all_to_all | solution.py:67
  741.5 2.5 fusion.2
  744.0 11.0 %all-to-all-done.1 = bf16[8,2,768]{2,1,0:T(2,128)(2,1)S(1)} async-done(((bf16[8,2,768]{2,1,0:T(2,128)(2,1)}), bf16[8,2,768]{2,1,0:T(2,128)(2,1)S(1)}, u32[]{:S(2)}, u32[]{:S(2)}) %all-to-all-start.1) | async-done | bytes 24608 | tf_op jit(solution)/shard_map/all_to_all | solution.py:67
  755.0 0.1 reshape.123
  755.1 0.1 copy.75
  755.3 0.9 gather_fusion
  756.1 0.4 multiply_reduce_fusion
  756.5 0.7 copy.82
  (22 shorter events, 0.2 us)
Async XLA Ops:
  7.2 59.3 %copy-start.4 = (bf16[256,172]{0,1:T(8,128)(2,1)S(1)}, bf16[256,172]{0,1:T(8,128)(2,1)}, u32[]{:S(2)}) copy-start(bf16[256,172]{0,1:T(8,128)(2,1)} %param.14) | copy-start | bytes 264196
  7.2 257.3 %all-gather.3.cloned.1.call-start = ((), (), s32[]{:S(2)}) async-start(), calls=%async_computation.4 | async-start | bytes 1597440 | tf_op jit(solution)/shard_map/all_gather | solution.py:50
  9.0 114.2 %copy-start.5 = (bf16[256,172]{0,1:T(8,128)(2,1)S(1)}, bf16[256,172]{0,1:T(8,128)(2,1)}, u32[]{:S(2)}) copy-start(bf16[256,172]{0,1:T(8,128)(2,1)} %param.15) | copy-start | bytes 264196
  44.0 146.3 %copy-start.6 = (bf16[172,256]{1,0:T(8,128)(2,1)S(1)}, bf16[172,256]{1,0:T(8,128)(2,1)}, u32[]{:S(2)}) copy-start(bf16[172,256]{1,0:T(8,128)(2,1)} %param.16) | copy-start | bytes 264196
  44.8 238.7 %all-gather.5.cloned.1.call-start = ((), (), s32[]{:S(2)}) async-start(), calls=%async_computation.6 | async-start | bytes 1597440 | tf_op jit(solution)/shard_map/all_gather | solution.py:51
  66.4 664.8 %reduce-scatter.2.cloned.1.call-start = ((), (), s32[]{:S(2)}) async-start(), calls=%async_computation.5 | async-start | bytes 3194880 | tf_op jit(solution)/shard_map/reduce_scatter | solution.py:58
  264.5 2.4 copy-start
  264.5 2.4 copy-start.8
  266.9 1.4 copy-start.3
  271.6 0.7 copy-start.7
  285.4 1.6 copy-start.2
  287.1 454.5 %copy-start.1 = (bf16[384,2048]{0,1:T(8,128)(2,1)S(1)}, bf16[384,2048]{0,1:T(8,128)(2,1)}, u32[]{:S(2)}) copy-start(bf16[384,2048]{0,1:T(8,128)(2,1)} %all-gather.5.cloned.1.call-done) | copy-start | bytes 4718596
  732.9 22.1 %all-to-all-start.1 = ((bf16[8,2,768]{2,1,0:T(2,128)(2,1)}), bf16[8,2,768]{2,1,0:T(2,128)(2,1)S(1)}, u32[]{:S(2)}, u32[]{:S(2)}) async-start(bf16[8,2,768]{2,1,0:T(2,128)(2,1)} %reshape.122), calls=%async_computation.2 | async-start | bytes 49152 | tf_op jit(solution)/shard_map/all_to_all | solution.py:67
Sparse Core Ops, SparseCore 0:
  44.9 113.7 all-gather.2
  161.5 121.9 all-gather.4
  286.3 444.9 reduce-scatter.1
where the time goes:
time: 764 us
  waiting for transfers between devices  465 us (61%)
  blocking collectives  247 us (32%)
  matrix products  14.7 us (2%)
  between operations  14 us (2%)
  local copies, waits for them, and re-layouts  11 us (1%)
  starting transfers between devices  8.76 us (1%)
    reduce_scatter x1, waiting for transfers between devices, local(): lax.psum_scatter(lax.dot_general(wide_down, hidden, (((0,), (1,)), ((), (...  443 us
    all_gather x1, blocking collectives, local(): down_full = lax.all_gather(dense_down, 'expert', axis=1, tiled=True)  74.2 us
    all_gather x1, blocking collectives, local(): lax.all_gather(dense_up, 'expert', axis=0, tiled=True)  67.1 us
    all_gather x1, blocking collectives, local(): lax.all_gather(dense_gate, 'expert', axis=0, tiled=True)  56.7 us
    all_to_all x1, blocking collectives, local(): lax.all_to_all(send_tok, 'expert', split_axis=0, concat_axis=0, tiled=True)  31.4 us
    all_to_all x1, blocking collectives, local(): lax.all_to_all(send_cot, 'expert', split_axis=0, concat_axis=0, tiled=True)  17.3 us
  transfers between devices with their start and end apart: 4, of which 3 were waited for; matrix products, arithmetic and copies ran while one was open for 2% of the time, Pallas kernels for 0%

commit v1 on v0

v1 whole, which is shorter than its diff:
```python
import jax
import jax.numpy as jnp
from jax import lax
from jax.experimental import pallas as pl
from jax.experimental.pallas import tpu as pltpu
from jax.sharding import Mesh, PartitionSpec as P

BF = jnp.bfloat16
F32 = jnp.float32
ZH, NX, NY, ZL, NC = 2, 4, 4, 8, 2
CAP = 48
SLOT = 128
NT = (((1,), (1,)), ((), ()))
VM = pl.BlockSpec(memory_space=pltpu.VMEM)
SM = pl.BlockSpec(memory_space=pltpu.SMEM)


def call(kernel, out_shape, in_specs, scratch=()):
    return pl.pallas_call(
        kernel,
        out_shape=out_shape,
        in_specs=in_specs,
        out_specs=jax.tree.map(lambda _: VM, out_shape),
        scratch_shapes=scratch,
        compiler_params=pltpu.CompilerParams(vmem_limit_bytes=60000 * 1024),
    )


def sds(shape, dtype):
    return jax.ShapeDtypeStruct(shape, dtype)


def select_kernel(zh_ref, r_ref, send_ref, pick_ref, wt_ref):
    zh = zh_ref[0]
    row8 = lax.broadcasted_iota(jnp.int32, (8, 128), 0)
    expert = jnp.where(row8 < NX, zh * NX + row8, -1).astype(F32)
    before = (
        lax.broadcasted_iota(jnp.int32, (128, 128), 0)
        < lax.broadcasted_iota(jnp.int32, (128, 128), 1)
    ).astype(F32).astype(BF)
    slot = lax.broadcasted_iota(jnp.int32, (CAP, 128), 0).astype(F32)
    pick_ref[...] = jnp.zeros_like(pick_ref)
    wt_ref[...] = jnp.zeros_like(wt_ref)
    for b in range(ZH):
        meta = r_ref[b * ZL, 64:72, :].astype(F32)
        id0, id1 = meta[0:1], meta[1:2]
        w0 = meta[2:3] + meta[3:4] + meta[4:5]
        w1 = meta[5:6] + meta[6:7] + meta[7:8]
        is0 = expert == id0
        is1 = expert == id1
        member = jnp.where(is0 | is1, 1.0, 0.0)
        weight = jnp.where(is0, w0, jnp.where(is1, w1, 0.0))
        earlier = jnp.dot(member.astype(BF), before, preferred_element_type=F32)
        wt_ref[b] = weight
        tok = r_ref[b * ZL : (b + 1) * ZL, 0:32, :].reshape(ZL * 32, 128)
        cot = r_ref[b * ZL : (b + 1) * ZL, 32:64, :].reshape(ZL * 32, 128)
        for x in range(NX):
            hit = jnp.where(
                (member[x : x + 1] > 0.5) & (earlier[x : x + 1] == slot), 1.0, 0.0
            )
            wslot = jnp.sum(hit * weight[x : x + 1], axis=1, keepdims=True)
            one = hit.astype(BF)
            pick_ref[b, x, b * CAP : (b + 1) * CAP, :] = one
            st = lax.dot_general(one, tok, NT, preferred_element_type=F32).astype(BF)
            sc = lax.dot_general(one, cot, NT, preferred_element_type=F32)
            sc = (sc * wslot).astype(BF)
            for y in range(NY):
                send_ref[x * NY + y, b * CAP : (b + 1) * CAP, 0:256] = st
                send_ref[x * NY + y, b * CAP : (b + 1) * CAP, 256:512] = sc


def main_kernel(
    c_ref, own_ref, oth_ref, w_ref, part_ref, away_ref, gg_ref, gu_ref, gd_ref, in_s, sg_s, o_s
):
    c = c_ref[0]
    j = lax.broadcasted_iota(jnp.int32, (512, 512), 0)
    f = lax.broadcasted_iota(jnp.int32, (512, 512), 1)
    core = (f >> 5) & 1
    src = jnp.where(core == c, 0, 256) + ((f >> 6) << 5) + (f & 31)
    perm = jnp.where(j == src, 1.0, 0.0).astype(BF)
    for x in range(NX):
        in_s[x * SLOT + 96 : (x + 1) * SLOT, :] = jnp.zeros((32, 2048), BF)
        sg_s[x * SLOT + 96 : (x + 1) * SLOT, :] = jnp.zeros((32, 2048), BF)
        for y in range(NY):
            k = x * NY + y
            for at, dst in ((0, in_s), (256, sg_s)):
                both = jnp.concatenate(
                    [own_ref[k, :, at : at + 256], oth_ref[k, :, at : at + 256]], axis=1
                )
                dst[x * SLOT : x * SLOT + 96, y * 512 : (y + 1) * 512] = jnp.dot(
                    both, perm, preferred_element_type=F32
                ).astype(BF)
    inp = in_s[...]
    sg = sg_s[...]
    gate = lax.dot_general(w_ref[0], inp, NT, preferred_element_type=F32)
    up = lax.dot_general(w_ref[1], inp, NT, preferred_element_type=F32)
    sig = jax.nn.sigmoid(gate)
    silu = gate * sig
    hidden = (silu * up).astype(BF)
    o_s[...] = lax.dot_general(
        w_ref[2], hidden, (((0,), (0,)), ((), ())), preferred_element_type=F32
    ).reshape(32, 2, 32, NX * SLOT)
    part_ref[...] = o_s[:, pl.ds(c, 1)].reshape(32, 32, NX * SLOT)
    away_ref[...] = o_s[:, pl.ds(1 - c, 1)].reshape(32, 32, NX * SLOT).astype(BF)
    gh = lax.dot_general(w_ref[2], sg, NT, preferred_element_type=F32)
    ggp = (gh * up * sig * (1.0 + gate * (1.0 - sig))).astype(BF)
    gup = (gh * silu).astype(BF)
    gg_ref[...] = jnp.dot(ggp, inp, preferred_element_type=F32).astype(BF)
    gu_ref[...] = jnp.dot(gup, inp, preferred_element_type=F32).astype(BF)
    gd_ref[...] = jnp.dot(hidden, sg, preferred_element_type=F32).astype(BF)


def add_kernel(part_ref, got_ref, send_ref):
    for x in range(NX):
        for y in range(NY):
            a = part_ref[y * ZL : (y + 1) * ZL, :, x * SLOT : (x + 1) * SLOT]
            b = got_ref[y * ZL : (y + 1) * ZL, :, x * SLOT : (x + 1) * SLOT]
            send_ref[x * NY + y] = (a + b.astype(F32)).astype(BF).reshape(256, SLOT)


def combine_kernel(r_ref, pick_ref, wt_ref, send_ref):
    acc = [jnp.zeros((256, 128), F32) for _ in range(ZH)]
    for x in range(NX):
        s = r_ref[x * NY].astype(F32)
        for y in range(1, NY):
            s = s + r_ref[x * NY + y].astype(F32)
        hi = s.astype(BF)
        lo = (s - hi.astype(F32)).astype(BF)
        for b in range(ZH):
            one = pick_ref[b, x]
            g = jnp.dot(hi, one, preferred_element_type=F32) + jnp.dot(
                lo, one, preferred_element_type=F32
            )
            acc[b] = acc[b] + g * wt_ref[b, x : x + 1, :]
    for b in range(ZH):
        send_ref[b * ZL : (b + 1) * ZL] = acc[b].astype(BF).reshape(ZL, 32, 128)


def last_kernel(r_ref, o_ref):
    s = r_ref[0].astype(F32)
    for k in range(1, ZH * ZL):
        s = s + r_ref[k].astype(F32)
    o_ref[...] = s.T.astype(BF)


def swap(v, axis):
    return lax.ppermute(v, axis, [(0, 1), (1, 0)])


def exchange(v, axes):
    return lax.all_to_all(v, axes, 0, 0, tiled=True)


def local(
    tokens,
    cotangent,
    expert_ids,
    route_weights,
    dense_gate,
    dense_up,
    dense_down,
    noise_gate,
    noise_up,
    noise_down,
):
    zh = lax.axis_index("zh")
    zh_arr = zh.reshape(1).astype(jnp.int32)
    c_arr = lax.axis_index("c").reshape(1).astype(jnp.int32)

    mine = jnp.stack([dense_gate.T, dense_up.T, dense_down])
    theirs = swap(mine, "zh")

    w_t = route_weights.T
    hi = lax.reduce_precision(w_t, 8, 7)
    mid = lax.reduce_precision(w_t - hi, 8, 7)
    low = w_t - hi - mid
    meta = jnp.concatenate(
        [
            expert_ids.T.astype(BF),
            jnp.stack([hi, mid, low], axis=1).reshape(6, 128).astype(BF),
        ],
        axis=0,
    )
    payload = jnp.concatenate([tokens.T, cotangent.T, meta], axis=0)
    got = exchange(jnp.broadcast_to(payload[None], (ZH * ZL, 72, 128)), ("zh", "zl"))

    send, pick, wt = call(
        select_kernel,
        (
            sds((NX * NY, 96, 512), BF),
            sds((ZH, NX, SLOT, 128), BF),
            sds((ZH, 8, 128), F32),
        ),
        [SM, VM],
    )(zh_arr, got)
    w_near = exchange(jnp.broadcast_to(mine[None], (NX, *mine.shape)), "x")
    own = exchange(send, ("x", "y"))
    w_far = exchange(jnp.broadcast_to(theirs[None], (NX, *mine.shape)), "x")
    oth = swap(own, "c")

    first = jnp.where(zh == 0, w_near, w_far)
    second = jnp.where(zh == 0, w_far, w_near)
    dense = jnp.concatenate([first, second], axis=0)
    dense = dense.transpose(1, 2, 0, 3).reshape(3, mine.shape[1], 2048)
    noise = jnp.stack([noise_gate[0].T, noise_up[0].T, noise_down[0]])
    wide = jnp.concatenate([dense, noise], axis=1)
    hid = wide.shape[1]

    part, away, gg, gu, gd = call(
        main_kernel,
        (
            sds((32, 32, NX * SLOT), F32),
            sds((32, 32, NX * SLOT), BF),
            sds((hid, 2048), BF),
            sds((hid, 2048), BF),
            sds((hid, 2048), BF),
        ),
        [SM, VM, VM, VM],
        [
            pltpu.VMEM((NX * SLOT, 2048), BF),
            pltpu.VMEM((NX * SLOT, 2048), BF),
            pltpu.VMEM((32, 2, 32, NX * SLOT), F32),
        ],
    )(c_arr, own, oth, wide)
    back = swap(away, "c")
    send = call(add_kernel, sds((NX * NY, 256, SLOT), BF), [VM, VM])(part, back)
    got = exchange(send, ("x", "y"))
    send = call(combine_kernel, sds((ZH * ZL, 32, 128), BF), [VM, VM, VM])(got, pick, wt)
    got = exchange(send, ("zh", "zl"))
    mixed = call(last_kernel, sds((128, 32), BF), [VM])(got)
    return mixed, gg[None], gu[None], gd[None]


def solution(mesh):
    e, s = ("zh", "x"), ("y", "zl", "c")
    fine = Mesh(mesh.devices.reshape(ZH, NX, NY, ZL, NC), e + s)
    in_specs = (
        P(e, s),
        P(e, s),
        P(e, None),
        P(e, None),
        P(e, s),
        P(e, s),
        P(s, e),
        P(e, None, s),
        P(e, None, s),
        P(e, s, None),
    )
    out_specs = (P(e, s), P(e, s, None), P(e, s, None), P(e, s, None))
    return jax.shard_map(local, mesh=fine, in_specs=in_specs, out_specs=out_specs, check_vma=False)
```

time: 764 us -> 192 us (0.25)
  the two profiles are of different devices: /device:TPU:2 before, /device:TPU:8 now
where the time goes in v1:
time: 192 us; the launch traced here: 191 us
  waiting for transfers between devices  62.3 us (32%)
  blocking collectives  48.3 us (25%)
  starting transfers between devices  43.9 us (23%)
  Pallas kernels  20.4 us (11%)
  local copies, waits for them, and re-layouts  10.4 us (5%)
  other arithmetic  5.11 us (3%)
    all_to_all x2, blocking collectives, exchange(): return lax.all_to_all(v, axes, 0, 0, tiled=True)  48.3 us
    all_to_all x4, waiting for transfers between devices, exchange(): return lax.all_to_all(v, axes, 0, 0, tiled=True)  37.9 us
    all_to_all x4, starting transfers between devices, exchange(): return lax.all_to_all(v, axes, 0, 0, tiled=True)  29.3 us
    ppermute x3, waiting for transfers between devices, swap(): return lax.ppermute(v, axis, [(0, 1), (1, 0)])  24.4 us
    ppermute x3, starting transfers between devices, swap(): return lax.ppermute(v, axis, [(0, 1), (1, 0)])  14.7 us
    pallas_call x1, Pallas kernels, local(): call(main_kernel, (sds((32, 32, NX * SLOT), F32), sds((32, 32, NX * SLOT)...  10.4 us
  transfers between devices with their start and end apart: 7, of which 5 were waited for; matrix products, arithmetic and copies ran while one was open for 4% of the time, Pallas kernels for 1%

profile of v1, /device:TPU:8, one launch (start us, length us, event | category | flops | bytes accessed | tf_op | source)
XLA Modules:
  0.0 191.2 jit_solution(7340664086853282561)
XLA Ops:
  0.6 0.7 convert_bitcast_fusion
  1.3 0.7 fusion.1
  2.0 0.7 pad_maximum_fusion.1
  2.8 0.8 broadcast_in_dim.12
  3.5 15.2 %all-to-all-start = ((bf16[16,72,128]{2,1,0:T(8,128)(2,1)}), bf16[16,72,128]{2,1,0:T(8,128)(2,1)S(1)}, u32[]{:S(2)}, u32[]{:S(2)}) async-start(bf16[16,72,128]{2,1,0:T(8,128)(2,1)} %broadcast_in_dim.12), calls=%async_computation | async-start | bytes 589824 | tf_op jit(solution)/shard_map/all_to_all | solution.py:151
  18.7 1.0 pad_maximum_fusion
  19.7 18.3 %all-to-all-done.r_ref = bf16[16,72,128]{2,1,0:T(8,128)(2,1)S(1)} async-done(((bf16[16,72,128]{2,1,0:T(8,128)(2,1)}), bf16[16,72,128]{2,1,0:T(8,128)(2,1)S(1)}, u32[]{:S(2)}, u32[]{:S(2)}) %all-to-all-start) | async-done | bytes 294944 | tf_op jit(solution)/shard_map/all_to_all | solution.py:151
  38.0 0.0 copy-start
  38.0 1.1 broadcast_in_dim.13
  39.1 4.3 %all-to-all-start.2 = ((bf16[4,3,172,256]{3,2,1,0:T(8,128)(2,1)}), bf16[4,3,172,256]{3,2,1,0:T(8,128)(2,1)S(1)}, u32[]{:S(2)}, u32[]{:S(2)}) async-start(bf16[4,3,172,256]{3,2,1,0:T(8,128)(2,1)} %broadcast_in_dim.13), calls=%async_computation.2 | async-start | bytes 2162688 | tf_op jit(solution)/shard_map/all_to_all | solution.py:151
  43.4 0.0 copy-done
  43.4 2.8 %shard_map.129 = (bf16[16,96,512]{2,1,0:T(8,128)(2,1)}, bf16[2,4,128,128]{3,2,1,0:T(8,128)(2,1)}, f32[2,8,128]{2,1,0:T(8,128)}) custom-call(s32[1]{0:T(128)} %bitcast.1.zh_ref, bf16[16,72,128]{2,1,0:T(8,128)(2,1)} %copy-done), custom_call_target="tpu_custom_call" | custom-call | tf_op jit(solution)/shard_map/pallas_call | solution.py:187
  46.2 8.2 %all-to-all-done.2 = bf16[4,3,172,256]{3,2,1,0:T(8,128)(2,1)S(1)} async-done(((bf16[4,3,172,256]{3,2,1,0:T(8,128)(2,1)}), bf16[4,3,172,256]{3,2,1,0:T(8,128)(2,1)S(1)}, u32[]{:S(2)}, u32[]{:S(2)}) %all-to-all-start.2) | async-done | bytes 1056800 | tf_op jit(solution)/shard_map/all_to_all | solution.py:151
  54.4 5.5 %all-to-all-start.1 = ((bf16[16,96,512]{2,1,0:T(8,128)(2,1)}), bf16[16,96,512]{2,1,0:T(8,128)(2,1)}, u32[]{:S(2)}, u32[]{:S(2)}) async-start(bf16[16,96,512]{2,1,0:T(8,128)(2,1)} %get-tuple-element.12), calls=%async_computation.1 | async-start | bytes 3145728 | tf_op jit(solution)/shard_map/all_to_all | solution.py:151
  60.0 10.8 %collective-permute-start.1 = (bf16[3,172,256]{2,1,0:T(8,128)(2,1)S(1)}, bf16[3,172,256]{2,1,0:T(8,128)(2,1)S(1)}, u32[]{:S(2)}, u32[]{:S(2)}) collective-permute-start(bf16[3,172,256]{2,1,0:T(8,128)(2,1)S(1)} %pad_maximum_fusion), channel_id=1, source_target_pairs={{0,256},{256,0},{1,257},{257,1},{2,258},{258,2},{3,259},{259,3},{4... | collective-permute-start | bytes 792584 | tf_op jit(solution)/shard_map/ppermute | solution.py:147
  70.8 21.6 %collective-permute-done.1 = bf16[3,172,256]{2,1,0:T(8,128)(2,1)S(1)} collective-permute-done((bf16[3,172,256]{2,1,0:T(8,128)(2,1)S(1)}, bf16[3,172,256]{2,1,0:T(8,128)(2,1)S(1)}, u32[]{:S(2)}, u32[]{:S(2)}) %collective-permute-start.1) | collective-permute-done | bytes 264224 | tf_op jit(solution)/shard_map/ppermute | solution.py:147
  92.4 0.0 all-to-all-done.1.own_ref
  92.4 1.1 broadcast_in_dim.14
  93.5 4.2 %all-to-all-start.3 = ((bf16[4,3,172,256]{3,2,1,0:T(8,128)(2,1)}), bf16[4,3,172,256]{3,2,1,0:T(8,128)(2,1)S(1)}, u32[]{:S(2)}, u32[]{:S(2)}) async-start(bf16[4,3,172,256]{3,2,1,0:T(8,128)(2,1)} %broadcast_in_dim.14), calls=%async_computation.3 | async-start | bytes 2162688 | tf_op jit(solution)/shard_map/all_to_all | solution.py:151
  97.7 1.9 collective-permute-start
  99.6 11.4 %all-to-all-done.3 = bf16[4,3,172,256]{3,2,1,0:T(8,128)(2,1)S(1)} async-done(((bf16[4,3,172,256]{3,2,1,0:T(8,128)(2,1)}), bf16[4,3,172,256]{3,2,1,0:T(8,128)(2,1)S(1)}, u32[]{:S(2)}, u32[]{:S(2)}) %all-to-all-start.3) | async-done | bytes 1056800 | tf_op jit(solution)/shard_map/all_to_all | solution.py:151
  111.0 0.1 broadcast_select_fusion.1
  111.2 0.2 maximum_bitcast_fusion
  111.4 2.1 %copy.18 = bf16[3,172,8,256]{3,2,1,0:T(8,128)(2,1)} copy(bf16[3,172,8,256]{3,1,0,2:T(8,128)(2,1)S(1)} %maximum_bitcast_fusion) | data formatting | bytes 4227072 | tf_op jit(solution)/shard_map/transpose | solution.py:204
  113.5 0.0 copy-start.2
  113.5 0.0 copy-start.3
  113.5 0.0 copy-start.4
  113.5 3.0 %reshape.24 = bf16[3,172,2048]{2,1,0:T(8,128)(2,1)S(1)} reshape(bf16[3,172,8,256]{3,2,1,0:T(8,128)(2,1)} %copy.18) | data formatting | bytes 4227072 | tf_op jit(solution)/shard_map/reshape | solution.py:204
  116.5 0.0 copy-done.2
  116.5 0.0 copy-done.3
  116.5 0.0 copy-done.4
  116.5 1.6 maximum_maximum_fusion.w_ref
  118.2 0.0 collective-permute-done.oth_ref
  118.2 10.4 %shard_map.130 = (f32[32,32,512]{2,1,0:T(8,128)}, bf16[32,32,512]{2,1,0:T(8,128)(2,1)}, bf16[192,2048]{1,0:T(8,128)(2,1)}, bf16[192,2048]{1,0:T(8,128)(2,1)}, bf16[192,2048]{1,0:T(8,128)(2,1)}) custom-call(s32[1]{0:T(128)} %bitcast.c_ref, bf16[16,96,512]{2,1,0:T(8,128)(2,1)} %all-to-all-done.1.own_ref, bf16[16,96,512]{2,1,0:T(8,128)(2,1)} %collective-permute-done.oth_ref, ...), custom_call_target="tpu_custom_call" | custom-call | tf_op jit(solution)/shard_map/pallas_call | solution.py:209
  128.6 1.9 collective-permute-start.2
  130.5 2.8 %collective-permute-done.2.got_ref = bf16[32,32,512]{2,1,0:T(8,128)(2,1)S(1)} collective-permute-done((bf16[32,32,512]{2,1,0:T(8,128)(2,1)}, bf16[32,32,512]{2,1,0:T(8,128)(2,1)S(1)}, u32[]{:S(2)}, u32[]{:S(2)}) %collective-permute-start.2) | collective-permute-done | bytes 1048608 | tf_op jit(solution)/shard_map/ppermute | solution.py:147
  133.3 0.0 copy-start.1
  133.3 1.0 copy-done.1
  134.3 3.1 %shard_map.131 = bf16[16,256,128]{2,1,0:T(8,128)(2,1)} custom-call(f32[32,32,512]{2,1,0:T(8,128)} %get-tuple-element.13.part_ref, bf16[32,32,512]{2,1,0:T(8,128)(2,1)} %copy-done.1), custom_call_target="tpu_custom_call" | custom-call | tf_op jit(solution)/shard_map/pallas_call | solution.py:226
  137.5 21.6 %all_to_all.30.r_ref = bf16[16,256,128]{2,1,0:T(8,128)(2,1)} all-to-all(bf16[16,256,128]{2,1,0:T(8,128)(2,1)} %shard_map.131), channel_id=1, replica_groups=mesh['zh'=2,'x'=4,'y'=4,'zl'=8,'c'=2] {'x','y'}, dimensions={0} | all-to-all | bytes 2097152 | tf_op jit(solution)/shard_map/all_to_all | solution.py:151
  159.0 2.4 %shard_map.132 = bf16[16,32,128]{2,1,0:T(8,128)(2,1)} custom-call(bf16[16,256,128]{2,1,0:T(8,128)(2,1)} %all_to_all.30.r_ref, bf16[2,4,128,128]{3,2,1,0:T(8,128)(2,1)} %get-tuple-element.15.pick_ref, f32[2,8,128]{2,1,0:T(8,128)} %get-tuple-element.16.wt_ref), custom_call_target="tpu_custom_call" | custom-call | tf_op jit(solution)/shard_map/pallas_call | solution.py:228
  161.4 26.7 %all_to_all.31.r_ref = bf16[16,32,128]{2,1,0:T(8,128)(2,1)} all-to-all(bf16[16,32,128]{2,1,0:T(8,128)(2,1)} %shard_map.132), channel_id=1, replica_groups=mesh['zh'=2,'x'=4,'y'=4,'zl'=8,'c'=2] {'zh','zl'}, dimensions={0} | all-to-all | bytes 262144 | tf_op jit(solution)/shard_map/all_to_all | solution.py:151
  188.2 1.6 shard_map.133
  189.8 1.4 copy.19
  (3 shorter events, 0.0 us)
Async XLA Ops:
  3.5 34.5 %all-to-all-start = ((bf16[16,72,128]{2,1,0:T(8,128)(2,1)}), bf16[16,72,128]{2,1,0:T(8,128)(2,1)S(1)}, u32[]{:S(2)}, u32[]{:S(2)}) async-start(bf16[16,72,128]{2,1,0:T(8,128)(2,1)} %broadcast_in_dim.12), calls=%async_computation | async-start | bytes 589824 | tf_op jit(solution)/shard_map/all_to_all | solution.py:151
  38.0 5.4 %copy-start = (bf16[16,72,128]{2,1,0:T(8,128)(2,1)}, bf16[16,72,128]{2,1,0:T(8,128)(2,1)S(1)}, u32[]{:S(2)}) copy-start(bf16[16,72,128]{2,1,0:T(8,128)(2,1)S(1)} %all-to-all-done.r_ref) | copy-start | bytes 884740
  39.1 15.4 %all-to-all-start.2 = ((bf16[4,3,172,256]{3,2,1,0:T(8,128)(2,1)}), bf16[4,3,172,256]{3,2,1,0:T(8,128)(2,1)S(1)}, u32[]{:S(2)}, u32[]{:S(2)}) async-start(bf16[4,3,172,256]{3,2,1,0:T(8,128)(2,1)} %broadcast_in_dim.13), calls=%async_computation.2 | async-start | bytes 2162688 | tf_op jit(solution)/shard_map/all_to_all | solution.py:151
  54.4 37.9 %all-to-all-start.1 = ((bf16[16,96,512]{2,1,0:T(8,128)(2,1)}), bf16[16,96,512]{2,1,0:T(8,128)(2,1)}, u32[]{:S(2)}, u32[]{:S(2)}) async-start(bf16[16,96,512]{2,1,0:T(8,128)(2,1)} %get-tuple-element.12), calls=%async_computation.1 | async-start | bytes 3145728 | tf_op jit(solution)/shard_map/all_to_all | solution.py:151
  60.0 32.4 %collective-permute-start.1 = (bf16[3,172,256]{2,1,0:T(8,128)(2,1)S(1)}, bf16[3,172,256]{2,1,0:T(8,128)(2,1)S(1)}, u32[]{:S(2)}, u32[]{:S(2)}) collective-permute-start(bf16[3,172,256]{2,1,0:T(8,128)(2,1)S(1)} %pad_maximum_fusion), channel_id=1, source_target_pairs={{0,256},{256,0},{1,257},{257,1},{2,258},{258,2},{3,259},{259,3},{4... | collective-permute-start | bytes 792584 | tf_op jit(solution)/shard_map/ppermute | solution.py:147
  93.5 17.6 %all-to-all-start.3 = ((bf16[4,3,172,256]{3,2,1,0:T(8,128)(2,1)}), bf16[4,3,172,256]{3,2,1,0:T(8,128)(2,1)S(1)}, u32[]{:S(2)}, u32[]{:S(2)}) async-start(bf16[4,3,172,256]{3,2,1,0:T(8,128)(2,1)} %broadcast_in_dim.14), calls=%async_computation.3 | async-start | bytes 2162688 | tf_op jit(solution)/shard_map/all_to_all | solution.py:151
  97.7 20.5 %collective-permute-start = (bf16[16,96,512]{2,1,0:T(8,128)(2,1)}, bf16[16,96,512]{2,1,0:T(8,128)(2,1)}, u32[]{:S(2)}, u32[]{:S(2)}) collective-permute-start(bf16[16,96,512]{2,1,0:T(8,128)(2,1)} %all-to-all-done.1.own_ref), channel_id=1, source_target_pairs={{0,1},{1,0},{2,3},{3,2},{4,5},{5,4},{6,7},{7,6},{8,9},{9,8},{10,11... | collective-permute-start | bytes 4718600 | tf_op jit(solution)/shard_map/ppermute | solution.py:147
  113.5 3.0 %copy-start.2 = (bf16[1,20,2048]{2,1,0:T(8,128)(2,1)S(1)}, bf16[1,20,2048]{2,1,0:T(8,128)(2,1)}, u32[]{:S(2)}) copy-start(bf16[1,20,2048]{2,1,0:T(8,128)(2,1)} %param.19) | copy-start | bytes 245764
  113.5 3.0 %copy-start.3 = (bf16[1,2048,20]{1,2,0:T(8,128)(2,1)S(1)}, bf16[1,2048,20]{1,2,0:T(8,128)(2,1)}, u32[]{:S(2)}) copy-start(bf16[1,2048,20]{1,2,0:T(8,128)(2,1)} %param.18) | copy-start | bytes 245764
  113.5 3.0 %copy-start.4 = (bf16[1,2048,20]{1,2,0:T(8,128)(2,1)S(1)}, bf16[1,2048,20]{1,2,0:T(8,128)(2,1)}, u32[]{:S(2)}) copy-start(bf16[1,2048,20]{1,2,0:T(8,128)(2,1)} %param.17) | copy-start | bytes 245764
  128.6 4.8 %collective-permute-start.2 = (bf16[32,32,512]{2,1,0:T(8,128)(2,1)}, bf16[32,32,512]{2,1,0:T(8,128)(2,1)S(1)}, u32[]{:S(2)}, u32[]{:S(2)}) collective-permute-start(bf16[32,32,512]{2,1,0:T(8,128)(2,1)} %get-tuple-element.14), channel_id=1, source_target_pairs={{0,1},{1,0},{2,3},{3,2},{4,5},{5,4},{6,7},{7,6},{8,9},{9,8},{10,11... | collective-permute-start | bytes 3145736 | tf_op jit(solution)/shard_map/ppermute | solution.py:147
  133.3 1.0 copy-start.1

commit v2 on v1

v2 whole, which is shorter than its diff:
```python
import jax
import jax.numpy as jnp
from jax import lax
from jax.experimental import pallas as pl
from jax.experimental.pallas import tpu as pltpu
from jax.sharding import Mesh, PartitionSpec as P

BF = jnp.bfloat16
F32 = jnp.float32
ZH, NX, NY, ZL, NC = 2, 4, 4, 8, 2
CAP = 48
ROWS = 2 * CAP
NT = (((1,), (1,)), ((), ()))
VM = pl.BlockSpec(memory_space=pltpu.VMEM)
SM = pl.BlockSpec(memory_space=pltpu.SMEM)


def call(kernel, out_shape, in_specs, scratch=(), mib=8, flops=0):
    return pl.pallas_call(
        kernel,
        out_shape=out_shape,
        in_specs=in_specs,
        out_specs=jax.tree.map(lambda _: VM, out_shape),
        scratch_shapes=scratch,
        compiler_params=pltpu.CompilerParams(vmem_limit_bytes=mib * 1024 * 1024),
    )


def sds(shape, dtype):
    return jax.ShapeDtypeStruct(shape, dtype)


def pack_kernel(tok_ref, cot_ref, id_ref, w_ref, a_ref):
    w = w_ref[...]
    high = w.astype(BF).astype(F32)
    mid = (w - high).astype(BF).astype(F32)
    low = w - high - mid
    meta = jnp.concatenate([id_ref[...].astype(F32), high, mid, low], axis=0).astype(BF)
    for k in range(ZH * ZL):
        a_ref[k, 0:32, :] = tok_ref[...]
        a_ref[k, 32:64, :] = cot_ref[...]
        a_ref[k, 64:72, :] = meta


def select_kernel(at_ref, r_ref, tok_ref, cot_ref, back_ref, ws_ref):
    zh = at_ref[0]
    row8 = lax.broadcasted_iota(jnp.int32, (8, 128), 0)
    expert = jnp.where(row8 < NX, zh * NX + row8, -1).astype(F32)
    before = (
        lax.broadcasted_iota(jnp.int32, (128, 128), 0)
        < lax.broadcasted_iota(jnp.int32, (128, 128), 1)
    ).astype(F32).astype(BF)
    slot = lax.broadcasted_iota(jnp.int32, (CAP, 128), 0).astype(F32)
    for b in range(ZH):
        meta = r_ref[b * ZL, 64:72, :].astype(F32)
        id0, id1 = meta[0:1], meta[1:2]
        w0 = meta[2:3] + meta[4:5] + meta[6:7]
        w1 = meta[3:4] + meta[5:6] + meta[7:8]
        is0 = expert == id0
        is1 = expert == id1
        member = jnp.where(is0 | is1, 1.0, 0.0)
        weight = jnp.where(is0, w0, jnp.where(is1, w1, 0.0))
        earlier = jnp.dot(member.astype(BF), before, preferred_element_type=F32)
        hits, ws = [], []
        for x in range(NX):
            hit = jnp.where(
                (member[x : x + 1] > 0.5) & (earlier[x : x + 1] == slot), 1.0, 0.0
            )
            hits.append(hit)
            ws.append(jnp.sum(hit * weight[x : x + 1], axis=1, keepdims=True))
        hit = jnp.concatenate(hits, axis=0)
        wslot = jnp.concatenate(ws, axis=0)
        one = hit.astype(BF)
        back_ref[b] = hit.T.astype(BF)
        ws_ref[b] = jnp.broadcast_to(wslot, (NX * CAP, 128))
        for at, scale, dst in ((0, None, tok_ref), (32, wslot, cot_ref)):
            v = r_ref[b * ZL : (b + 1) * ZL, at : at + 32, :].reshape(ZL * 32, 128)
            v = lax.dot_general(one, v, NT, preferred_element_type=F32)
            v = (v if scale is None else v * scale).astype(BF)
            for x in range(NX):
                for y in range(NY):
                    dst[x * NY + y, b * CAP : (b + 1) * CAP, :] = v[x * CAP : (x + 1) * CAP]


def spread(c):
    j = lax.broadcasted_iota(jnp.int32, (512, 512), 0)
    f = lax.broadcasted_iota(jnp.int32, (512, 512), 1)
    src = jnp.where(((f >> 5) & 1) == c, 0, 256) + ((f >> 6) << 5) + (f & 31)
    return jnp.where(j == src, 1.0, 0.0).astype(BF)


def join(own_ref, oth_ref, perm, dst):
    for y in range(NY):
        rows = jnp.concatenate(
            [
                jnp.concatenate([own_ref[x * NY + y], oth_ref[x * NY + y]], axis=1)
                for x in range(NX)
            ],
            axis=0,
        )
        dst[:, y * 512 : (y + 1) * 512] = jnp.dot(
            rows, perm, preferred_element_type=F32
        ).astype(BF)


HID = 208
DENSE, NEW_AT, NEW = 172, 176, 20


def forward_kernel(
    at_ref, own_ref, oth_ref, n0, n1, n2, n3, f0, f1, f2, f3, ng_ref, nu_ref, nd_ref,
    part_ref, away_ref, in_ref, gu_ref, hid_ref, down_ref, w_s,
):
    zh, c, at_x = at_ref[0], at_ref[1], at_ref[2]
    perm = spread(c)
    join(own_ref, oth_ref, perm, in_ref)
    for m, new in ((0, ng_ref), (1, nu_ref)):
        w_s[m, 160:HID, :] = jnp.zeros((HID - 160, 2048), BF)
        w_s[m, NEW_AT : NEW_AT + NEW, :] = new[...]
    down_ref[160:HID, :] = jnp.zeros((HID - 160, 2048), BF)
    down_ref[NEW_AT : NEW_AT + NEW, :] = nd_ref[...]
    for half, refs in ((zh, (n0, n1, n2, n3)), (1 - zh, (f0, f1, f2, f3))):
        for k, ref in enumerate(refs):
            source = half * NX + ((at_x + NX - k) & (NX - 1))
            lanes = pl.ds(pl.multiple_of(source * 256, 256), 256)
            w_s[0, 0:DENSE, lanes] = ref[0]
            w_s[1, 0:DENSE, lanes] = ref[1]
            down_ref[0:DENSE, lanes] = ref[2]
    gu = lax.dot_general(
        w_s[...].reshape(2 * HID, 2048), in_ref[...], NT, preferred_element_type=F32
    )
    gu_ref[...] = gu
    gate, up = gu[0:HID], gu[HID : 2 * HID]
    hidden = gate * jax.nn.sigmoid(gate) * up
    hid_ref[...] = hidden.astype(BF)
    rows = hidden.T.astype(BF)
    for y in range(NY):
        d = lax.dot_general(
            down_ref[:, y * 512 : (y + 1) * 512], perm, NT, preferred_element_type=F32
        ).astype(BF)
        o = jnp.dot(rows, d, preferred_element_type=F32)
        for x in range(NX):
            part_ref[x * NY + y] = o[x * ROWS : (x + 1) * ROWS, 0:256]
            away_ref[x * NY + y] = o[x * ROWS : (x + 1) * ROWS, 256:512].astype(BF)


def grad_kernel(
    at_ref, own_ref, oth_ref, in_ref, gu_ref, hid_ref, down_ref, gg_ref, gup_ref, gd_ref, sg_s
):
    join(own_ref, oth_ref, spread(at_ref[1]), sg_s)
    sg = sg_s[...]
    inp = in_ref[...]
    gate, up = gu_ref[0:HID], gu_ref[HID : 2 * HID]
    sig = jax.nn.sigmoid(gate)
    gh = lax.dot_general(down_ref[...], sg, NT, preferred_element_type=F32)
    ggp = (gh * up * sig * (1.0 + gate * (1.0 - sig))).astype(BF)
    gup = (gh * (gate * sig)).astype(BF)
    for lhs, rhs, out in ((ggp, inp, gg_ref), (gup, inp, gup_ref), (hid_ref[...], sg, gd_ref)):
        g = jnp.dot(lhs, rhs, preferred_element_type=F32).astype(BF)
        out[0:DENSE, :] = g[0:DENSE]
        out[DENSE : DENSE + NEW, :] = g[NEW_AT : NEW_AT + NEW]


def combine_kernel(r_ref, back_ref, ws_ref, send_ref):
    sums = []
    for x in range(NX):
        s = r_ref[x * NY].astype(F32)
        for y in range(1, NY):
            s = s + r_ref[x * NY + y].astype(F32)
        sums.append(s)
    for b in range(ZH):
        s = jnp.concatenate([v[b * CAP : (b + 1) * CAP] for v in sums], axis=0)
        s = s * ws_ref[b, :, 0:1]
        hi = s.astype(BF)
        lo = (s - hi.astype(F32)).astype(BF)
        m = jnp.dot(back_ref[b], hi, preferred_element_type=F32) + jnp.dot(
            back_ref[b], lo, preferred_element_type=F32
        )
        send_ref[b * ZL : (b + 1) * ZL] = m.T.astype(BF).reshape(ZL, 32, 128)


def swap(v, axis):
    return lax.ppermute(v, axis, [(0, 1), (1, 0)])


def turn(v, k):
    return lax.ppermute(v, "x", [(i, (i + k) % NX) for i in range(NX)])


def exchange(v, axes):
    return lax.all_to_all(v, axes, 0, 0, tiled=True)


def local(
    tokens,
    cotangent,
    expert_ids,
    route_weights,
    dense_gate,
    dense_up,
    dense_down,
    noise_gate,
    noise_up,
    noise_down,
):
    Z, XY = ("zh", "zl"), ("x", "y")
    at = jnp.stack([lax.axis_index(n) for n in ("zh", "c", "x")]).astype(jnp.int32)
    hid = dense_down.shape[0] + noise_down.shape[1]

    mine = jnp.stack([dense_gate.T, dense_up.T, dense_down])
    theirs = swap(mine, "zh")
    payload = call(pack_kernel, sds((16, 72, 128), BF), [VM] * 4)(
        tokens.T, cotangent.T, expert_ids.T, route_weights.T
    )
    near = [mine] + [turn(mine, k) for k in range(1, NX)]
    got = exchange(payload, Z)
    got, theirs, near = lax.optimization_barrier((got, theirs, near))
    tok_send, cot_send, back, ws = call(
        select_kernel,
        (
            sds((16, ROWS, 256), BF),
            sds((16, ROWS, 256), BF),
            sds((ZH, 128, NX * CAP), BF),
            sds((ZH, NX * CAP, 128), F32),
        ),
        [SM, VM],
    )(at, got)
    own = exchange(tok_send, XY)
    far = [theirs] + [turn(theirs, k) for k in range(1, NX)]
    oth = swap(own, "c")
    cot_send, _ = lax.optimization_barrier((cot_send, own))
    own_cot = exchange(cot_send, XY)
    oth_cot = swap(own_cot, "c")

    part, away, inp, gu, hidden, down = call(
        forward_kernel,
        (
            sds((16, ROWS, 256), F32),
            sds((16, ROWS, 256), BF),
            sds((NX * ROWS, 2048), BF),
            sds((2 * HID, NX * ROWS), F32),
            sds((HID, NX * ROWS), BF),
            sds((HID, 2048), BF),
        ),
        [SM] + [VM] * 13,
        [pltpu.VMEM((2, HID, 2048), BF)],
        mib=28,
    )(at, own, oth, *near, *far, noise_gate[0].T, noise_up[0].T, noise_down[0])
    send = (part + swap(away, "c").astype(F32)).astype(BF)
    own_cot, oth_cot, send = lax.optimization_barrier((own_cot, oth_cot, send))
    gg, gup, gd = call(
        grad_kernel,
        (sds((hid, 2048), BF),) * 3,
        [SM] + [VM] * 6,
        [pltpu.VMEM((NX * ROWS, 2048), BF)],
        mib=28,
    )(at, own_cot, oth_cot, inp, gu, hidden, down)
    got = exchange(send, XY)
    send = call(combine_kernel, sds((16, 32, 128), BF), [VM] * 3)(got, back, ws)
    got = exchange(send, Z)
    mixed = jnp.sum(got.astype(F32), axis=0).astype(BF).T
    return mixed, gg[None], gup[None], gd[None]


def solution(mesh):
    e, s = ("zh", "x"), ("y", "zl", "c")
    fine = Mesh(mesh.devices.reshape(ZH, NX, NY, ZL, NC), e + s)
    in_specs = (
        P(e, s),
        P(e, s),
        P(e, None),
        P(e, None),
        P(e, s),
        P(e, s),
        P(s, e),
        P(e, None, s),
        P(e, None, s),
        P(e, s, None),
    )
    out_specs = (P(e, s), P(e, s, None), P(e, s, None), P(e, s, None))
    return jax.shard_map(local, mesh=fine, in_specs=in_specs, out_specs=out_specs, check_vma=False)
```

time: 192 us -> 183 us (0.953)
  the two profiles are of different devices: /device:TPU:8 before, /device:TPU:32 now
where the time goes in v2:
time: 183 us; the launch traced here: 182 us
  starting transfers between devices  64.2 us (35%)
  waiting for transfers between devices  41.7 us (23%)
  blocking collectives  40.3 us (22%)
  local copies, waits for them, and re-layouts  18.5 us (10%)
  Pallas kernels  13.3 us (7%)
  other arithmetic  3.08 us (2%)
    all_to_all x2, blocking collectives, exchange(): return lax.all_to_all(v, axes, 0, 0, tiled=True)  40.3 us
    all_to_all x3, starting transfers between devices, exchange(): return lax.all_to_all(v, axes, 0, 0, tiled=True)  23.7 us
    ppermute x6, starting transfers between devices, turn(): return lax.ppermute(v, 'x', [(i, (i + k) % NX) for i in range(NX)])  23.2 us
    ppermute x4, waiting for transfers between devices, swap(): return lax.ppermute(v, axis, [(0, 1), (1, 0)])  22.2 us
    unnamed x54, local copies, waits for them, and re-layouts  18.5 us
    ppermute x4, starting transfers between devices, swap(): return lax.ppermute(v, axis, [(0, 1), (1, 0)])  17.4 us
    ppermute x6, waiting for transfers between devices, turn(): return lax.ppermute(v, 'x', [(i, (i + k) % NX) for i in range(NX)])  12.8 us
    all_to_all x3, waiting for transfers between devices, exchange(): return lax.all_to_all(v, axes, 0, 0, tiled=True)  6.68 us
  transfers between devices with their start and end apart: 13, of which 6 were waited for; matrix products, arithmetic and copies ran while one was open for 1% of the time, Pallas kernels for 5%

profile of v2, /device:TPU:32, one launch (start us, length us, event | category | flops | bytes accessed | tf_op | source)
XLA Modules:
  0.0 182.0 jit_solution(3989326693811082862)
XLA Ops:
  0.6 0.0 copy-start.23
  0.6 0.7 copy-done.23
  1.3 0.7 copy-done.24
  2.0 0.7 copy-done.25
  2.7 0.7 copy-done.26
  3.4 0.8 shard_map.129
  4.1 15.2 %all-to-all-start = ((bf16[16,72,128]{2,1,0:T(8,128)(2,1)}), bf16[16,72,128]{2,1,0:T(8,128)(2,1)S(1)}, u32[]{:S(2)}, u32[]{:S(2)}) async-start(bf16[16,72,128]{2,1,0:T(8,128)(2,1)} %shard_map.129), calls=%async_computation | async-start | bytes 589824 | tf_op jit(solution)/shard_map/all_to_all | solution.py:191
  19.4 1.0 pad_maximum_fusion.n0
  20.4 11.2 %collective-permute-start = (bf16[3,172,256]{2,1,0:T(8,128)(2,1)S(1)}, bf16[3,172,256]{2,1,0:T(8,128)(2,1)S(1)}, u32[]{:S(2)}, u32[]{:S(2)}) collective-permute-start(bf16[3,172,256]{2,1,0:T(8,128)(2,1)S(1)} %pad_maximum_fusion.n0), channel_id=1, source_target_pairs={{0,256},{256,0},{1,257},{257,1},{2,258},{258,2},{3,259},{259,3},{4... | collective-permute-start | bytes 792584 | tf_op jit(solution)/shard_map/ppermute | solution.py:183
  31.6 3.4 %collective-permute-start.1 = (bf16[3,172,256]{2,1,0:T(8,128)(2,1)S(1)}, bf16[3,172,256]{2,1,0:T(8,128)(2,1)S(1)}, u32[]{:S(2)}, u32[]{:S(2)}) collective-permute-start(bf16[3,172,256]{2,1,0:T(8,128)(2,1)S(1)} %pad_maximum_fusion.n0), channel_id=1, source_target_pairs={{0,64},{64,128},{128,192},{192,0},{1,65},{65,129},{129,193},{193,1... | collective-permute-start | bytes 792584 | tf_op jit(solution)/shard_map/ppermute | solution.py:187
  35.0 4.6 %collective-permute-start.2 = (bf16[3,172,256]{2,1,0:T(8,128)(2,1)S(1)}, bf16[3,172,256]{2,1,0:T(8,128)(2,1)S(1)}, u32[]{:S(2)}, u32[]{:S(2)}) collective-permute-start(bf16[3,172,256]{2,1,0:T(8,128)(2,1)S(1)} %pad_maximum_fusion.n0), channel_id=1, source_target_pairs={{0,128},{64,192},{128,0},{192,64},{1,129},{65,193},{129,1},{193,65... | collective-permute-start | bytes 792584 | tf_op jit(solution)/shard_map/ppermute | solution.py:187
  39.6 3.3 %collective-permute-start.3 = (bf16[3,172,256]{2,1,0:T(8,128)(2,1)S(1)}, bf16[3,172,256]{2,1,0:T(8,128)(2,1)S(1)}, u32[]{:S(2)}, u32[]{:S(2)}) collective-permute-start(bf16[3,172,256]{2,1,0:T(8,128)(2,1)S(1)} %pad_maximum_fusion.n0), channel_id=1, source_target_pairs={{0,192},{64,0},{128,64},{192,128},{1,193},{65,1},{129,65},{193,129... | collective-permute-start | bytes 792584 | tf_op jit(solution)/shard_map/ppermute | solution.py:187
  43.0 0.1 pad_add_fusion.at_ref
  43.1 21.7 %collective-permute-done.f0 = bf16[3,172,256]{2,1,0:T(8,128)(2,1)S(1)} collective-permute-done((bf16[3,172,256]{2,1,0:T(8,128)(2,1)S(1)}, bf16[3,172,256]{2,1,0:T(8,128)(2,1)S(1)}, u32[]{:S(2)}, u32[]{:S(2)}) %collective-permute-start) | collective-permute-done | bytes 264224 | tf_op jit(solution)/shard_map/ppermute | solution.py:183
  64.8 0.0 collective-permute-done.1.n1
  64.8 0.0 collective-permute-done.2.n2
  64.8 0.7 copy-done.12
  65.5 0.0 collective-permute-done.3.n3
  65.5 0.7 copy-done.14
  66.2 0.0 all-to-all-done.r_ref
  66.2 2.0 %shard_map.130 = (bf16[16,96,256]{2,1,0:T(8,128)(2,1)S(1)}, bf16[16,96,256]{2,1,0:T(8,128)(2,1)}, bf16[2,128,192]{2,1,0:T(8,128)(2,1)S(1)}, f32[2,192,128]{2,1,0:T(8,128)S(1)}) custom-call(s32[3]{0:T(128)S(1)} %pad_add_fusion.at_ref, bf16[16,72,128]{2,1,0:T(8,128)(2,1)S(1)} %all-to-all-done.r_ref), custom_call_target="tpu_custom_call" | custom-call | tf_op jit(solution)/shard_map/pallas_call | solution.py:218
  68.2 20.8 %all_to_all.25.own_ref = bf16[16,96,256]{2,1,0:T(8,128)(2,1)S(1)} all-to-all(bf16[16,96,256]{2,1,0:T(8,128)(2,1)S(1)} %get-tuple-element.29), channel_id=1, replica_groups=mesh['zh'=2,'x'=4,'y'=4,'zl'=8,'c'=2] {'x','y'}, dimensions={0} | all-to-all | bytes 1572864 | tf_op jit(solution)/shard_map/all_to_all | solution.py:191
  89.0 1.9 %collective-permute-start.5 = (bf16[16,96,256]{2,1,0:T(8,128)(2,1)S(1)}, bf16[16,96,256]{2,1,0:T(8,128)(2,1)S(1)}, u32[]{:S(2)}, u32[]{:S(2)}) collective-permute-start(bf16[16,96,256]{2,1,0:T(8,128)(2,1)S(1)} %all_to_all.25.own_ref), channel_id=1, source_target_pairs={{0,1},{1,0},{2,3},{3,2},{4,5},{5,4},{6,7},{7,6},{8,9},{9,8},{10,11... | collective-permute-start | bytes 2359304 | tf_op jit(solution)/shard_map/ppermute | solution.py:183
  90.9 3.7 %all-to-all-start.2 = ((bf16[16,96,256]{2,1,0:T(8,128)(2,1)}), bf16[16,96,256]{2,1,0:T(8,128)(2,1)S(1)}, u32[]{:S(2)}, u32[]{:S(2)}) async-start(bf16[16,96,256]{2,1,0:T(8,128)(2,1)} %get-tuple-element.30), calls=%async_computation.2 | async-start | bytes 1572864 | tf_op jit(solution)/shard_map/all_to_all | solution.py:191
  94.6 3.8 %collective-permute-start.6 = (bf16[3,172,256]{2,1,0:T(8,128)(2,1)S(1)}, bf16[3,172,256]{2,1,0:T(8,128)(2,1)S(1)}, u32[]{:S(2)}, u32[]{:S(2)}) collective-permute-start(bf16[3,172,256]{2,1,0:T(8,128)(2,1)S(1)} %collective-permute-done.f0), channel_id=1, source_target_pairs={{0,64},{64,128},{128,192},{192,0},{1,65},{65,129},{129,193},{193,1... | collective-permute-start | bytes 792584 | tf_op jit(solution)/shard_map/ppermute | solution.py:187
  98.5 4.6 %collective-permute-start.7 = (bf16[3,172,256]{2,1,0:T(8,128)(2,1)S(1)}, bf16[3,172,256]{2,1,0:T(8,128)(2,1)S(1)}, u32[]{:S(2)}, u32[]{:S(2)}) collective-permute-start(bf16[3,172,256]{2,1,0:T(8,128)(2,1)S(1)} %collective-permute-done.f0), channel_id=1, source_target_pairs={{0,128},{64,192},{128,0},{192,64},{1,129},{65,193},{129,1},{193,65... | collective-permute-start | bytes 792584 | tf_op jit(solution)/shard_map/ppermute | solution.py:187
  103.1 3.4 %collective-permute-start.8 = (bf16[3,172,256]{2,1,0:T(8,128)(2,1)S(1)}, bf16[3,172,256]{2,1,0:T(8,128)(2,1)S(1)}, u32[]{:S(2)}, u32[]{:S(2)}) collective-permute-start(bf16[3,172,256]{2,1,0:T(8,128)(2,1)S(1)} %collective-permute-done.f0), channel_id=1, source_target_pairs={{0,192},{64,0},{128,64},{192,128},{1,193},{65,1},{129,65},{193,129... | collective-permute-start | bytes 792584 | tf_op jit(solution)/shard_map/ppermute | solution.py:187
  106.5 6.9 %collective-permute-done.6.f1 = bf16[3,172,256]{2,1,0:T(8,128)(2,1)S(1)} collective-permute-done((bf16[3,172,256]{2,1,0:T(8,128)(2,1)S(1)}, bf16[3,172,256]{2,1,0:T(8,128)(2,1)S(1)}, u32[]{:S(2)}, u32[]{:S(2)}) %collective-permute-start.6) | collective-permute-done | bytes 264224 | tf_op jit(solution)/shard_map/ppermute | solution.py:187
  113.4 5.9 %collective-permute-done.7.f2 = bf16[3,172,256]{2,1,0:T(8,128)(2,1)S(1)} collective-permute-done((bf16[3,172,256]{2,1,0:T(8,128)(2,1)S(1)}, bf16[3,172,256]{2,1,0:T(8,128)(2,1)S(1)}, u32[]{:S(2)}, u32[]{:S(2)}) %collective-permute-start.7) | collective-permute-done | bytes 264224 | tf_op jit(solution)/shard_map/ppermute | solution.py:187
  119.3 0.0 collective-permute-done.8.f3
  119.3 0.0 collective-permute-done.5.oth_ref
  119.3 0.9 copy-done.4
  120.1 1.1 copy-done.5
  121.3 1.0 copy-done.9
  122.2 1.0 copy-done.11
  123.2 1.0 copy-done.13
  124.1 1.0 copy-done.15
  125.1 0.9 copy-done.20
  126.0 0.9 copy-done.21
  126.9 0.9 copy-done.22
  127.8 5.0 %shard_map.131 = (f32[16,96,256]{2,1,0:T(8,128)S(1)}, bf16[16,96,256]{2,1,0:T(8,128)(2,1)}, bf16[384,2048]{1,0:T(8,128)(2,1)S(1)}, f32[416,384]{1,0:T(8,128)S(1)...) custom-call(s32[3]{0:T(128)S(1)} %pad_add_fusion.at_ref, bf16[16,96,256]{2,1,0:T(8,128)(2,1)S(1)} %all_to_all.25.own_ref, ...), custom_call_target="tpu_custom_call" | custom-call | tf_op jit(solution)/shard_map/pallas_call | solution.py:235
  132.8 1.2 copy-done
  134.0 0.9 copy-done.2
  134.9 0.8 copy-done.6
  135.7 0.7 copy-done.18
  136.4 1.9 %collective-permute-start.9 = (bf16[16,96,256]{2,1,0:T(8,128)(2,1)}, bf16[16,96,256]{2,1,0:T(8,128)(2,1)}, u32[]{:S(2)}, u32[]{:S(2)}) collective-permute-start(bf16[16,96,256]{2,1,0:T(8,128)(2,1)} %get-tuple-element.37), channel_id=1, source_target_pairs={{0,1},{1,0},{2,3},{3,2},{4,5},{5,4},{6,7},{7,6},{8,9},{9,8},{10,11... | collective-permute-start | bytes 2359304 | tf_op jit(solution)/shard_map/ppermute | solution.py:183
  138.3 0.0 all-to-all-done.2.own_ref
  138.3 2.4 %collective-permute-start.4 = (bf16[16,96,256]{2,1,0:T(8,128)(2,1)S(1)}, bf16[16,96,256]{2,1,0:T(8,128)(2,1)S(1)}, u32[]{:S(2)}, u32[]{:S(2)}) collective-permute-start(bf16[16,96,256]{2,1,0:T(8,128)(2,1)S(1)} %all-to-all-done.2.own_ref), channel_id=1, source_target_pairs={{0,1},{1,0},{2,3},{3,2},{4,5},{5,4},{6,7},{7,6},{8,9},{9,8},{10,11... | collective-permute-start | bytes 2359304 | tf_op jit(solution)/shard_map/ppermute | solution.py:183
  140.7 0.2 collective-permute-done.9
  140.9 1.4 add_convert_fusion
  142.3 0.0 copy-start.1
  142.3 0.0 copy-start.19
  142.3 0.3 collective-permute-done.4.oth_ref
  142.6 19.5 %all_to_all.26.r_ref = bf16[16,96,256]{2,1,0:T(8,128)(2,1)S(1)} all-to-all(bf16[16,96,256]{2,1,0:T(8,128)(2,1)S(1)} %add_convert_fusion), channel_id=1, replica_groups=mesh['zh'=2,'x'=4,'y'=4,'zl'=8,'c'=2] {'x','y'}, dimensions={0} | all-to-all | bytes 1572864 | tf_op jit(solution)/shard_map/all_to_all | solution.py:191
  162.2 1.1 shard_map.132
  163.2 4.8 %all-to-all-start.4 = ((bf16[16,32,128]{2,1,0:T(8,128)(2,1)}), bf16[16,32,128]{2,1,0:T(8,128)(2,1)S(1)}, u32[]{:S(2)}, u32[]{:S(2)}) async-start(bf16[16,32,128]{2,1,0:T(8,128)(2,1)} %shard_map.132), calls=%async_computation.4 | async-start | bytes 262144 | tf_op jit(solution)/shard_map/all_to_all | solution.py:191
  168.0 0.0 copy-done.1
  168.0 0.0 copy-done.19
  168.0 0.0 copy-start.3
  168.0 1.1 copy-done.3
  169.2 1.1 copy-done.7
  170.3 4.4 %shard_map.133 = (bf16[192,2048]{1,0:T(8,128)(2,1)}, bf16[192,2048]{1,0:T(8,128)(2,1)}, bf16[192,2048]{1,0:T(8,128)(2,1)}) custom-call(s32[3]{0:T(128)S(1)} %pad_add_fusion.at_ref, bf16[16,96,256]{2,1,0:T(8,128)(2,1)S(1)} %all-to-all-done.2.own_ref, bf16[16,96,256]{2,1,0:T(8,128)(2,1)S(1)} %collective-permute-done.4.oth_ref, ...), custom_call_target="tpu_custom_call" | custom-call | tf_op jit(solution)/shard_map/pallas_call | solution.py:251
  174.7 6.7 %all-to-all-done.4 = bf16[16,32,128]{2,1,0:T(8,128)(2,1)S(1)} async-done(((bf16[16,32,128]{2,1,0:T(8,128)(2,1)}), bf16[16,32,128]{2,1,0:T(8,128)(2,1)S(1)}, u32[]{:S(2)}, u32[]{:S(2)}) %all-to-all-start.4) | async-done | bytes 131104 | tf_op jit(solution)/shard_map/all_to_all | solution.py:191
  181.3 0.6 reduce_sum.12
  (27 shorter events, 0.0 us)
Async XLA Ops:
  0.6 0.7 copy-start.23
  1.3 0.7 copy-start.24
  2.0 0.7 copy-start.25
  2.7 0.7 copy-start.26
  4.1 62.1 %all-to-all-start = ((bf16[16,72,128]{2,1,0:T(8,128)(2,1)}), bf16[16,72,128]{2,1,0:T(8,128)(2,1)S(1)}, u32[]{:S(2)}, u32[]{:S(2)}) async-start(bf16[16,72,128]{2,1,0:T(8,128)(2,1)} %shard_map.129), calls=%async_computation | async-start | bytes 589824 | tf_op jit(solution)/shard_map/all_to_all | solution.py:191
  20.4 44.4 %collective-permute-start = (bf16[3,172,256]{2,1,0:T(8,128)(2,1)S(1)}, bf16[3,172,256]{2,1,0:T(8,128)(2,1)S(1)}, u32[]{:S(2)}, u32[]{:S(2)}) collective-permute-start(bf16[3,172,256]{2,1,0:T(8,128)(2,1)S(1)} %pad_maximum_fusion.n0), channel_id=1, source_target_pairs={{0,256},{256,0},{1,257},{257,1},{2,258},{258,2},{3,259},{259,3},{4... | collective-permute-start | bytes 792584 | tf_op jit(solution)/shard_map/ppermute | solution.py:183
  31.6 33.2 %collective-permute-start.1 = (bf16[3,172,256]{2,1,0:T(8,128)(2,1)S(1)}, bf16[3,172,256]{2,1,0:T(8,128)(2,1)S(1)}, u32[]{:S(2)}, u32[]{:S(2)}) collective-permute-start(bf16[3,172,256]{2,1,0:T(8,128)(2,1)S(1)} %pad_maximum_fusion.n0), channel_id=1, source_target_pairs={{0,64},{64,128},{128,192},{192,0},{1,65},{65,129},{129,193},{193,1... | collective-permute-start | bytes 792584 | tf_op jit(solution)/shard_map/ppermute | solution.py:187
  35.0 29.8 %collective-permute-start.2 = (bf16[3,172,256]{2,1,0:T(8,128)(2,1)S(1)}, bf16[3,172,256]{2,1,0:T(8,128)(2,1)S(1)}, u32[]{:S(2)}, u32[]{:S(2)}) collective-permute-start(bf16[3,172,256]{2,1,0:T(8,128)(2,1)S(1)} %pad_maximum_fusion.n0), channel_id=1, source_target_pairs={{0,128},{64,192},{128,0},{192,64},{1,129},{65,193},{129,1},{193,65... | collective-permute-start | bytes 792584 | tf_op jit(solution)/shard_map/ppermute | solution.py:187
  39.6 25.9 %collective-permute-start.3 = (bf16[3,172,256]{2,1,0:T(8,128)(2,1)S(1)}, bf16[3,172,256]{2,1,0:T(8,128)(2,1)S(1)}, u32[]{:S(2)}, u32[]{:S(2)}) collective-permute-start(bf16[3,172,256]{2,1,0:T(8,128)(2,1)S(1)} %pad_maximum_fusion.n0), channel_id=1, source_target_pairs={{0,192},{64,0},{128,64},{192,128},{1,193},{65,1},{129,65},{193,129... | collective-permute-start | bytes 792584 | tf_op jit(solution)/shard_map/ppermute | solution.py:187
  64.8 38.3 %copy-start.8 = (bf16[3,172,256]{2,1,0:T(8,128)(2,1)}, bf16[3,172,256]{2,1,0:T(8,128)(2,1)S(1)}, u32[]{:S(2)}) copy-start(bf16[3,172,256]{2,1,0:T(8,128)(2,1)S(1)} %collective-permute-done.f0) | copy-start | bytes 792580
  64.8 26.1 %copy-start.10 = (bf16[3,172,256]{2,1,0:T(8,128)(2,1)}, bf16[3,172,256]{2,1,0:T(8,128)(2,1)S(1)}, u32[]{:S(2)}) copy-start(bf16[3,172,256]{2,1,0:T(8,128)(2,1)S(1)} %collective-permute-done.1.n1) | copy-start | bytes 792580
  64.8 0.7 copy-start.12
  65.5 0.7 copy-start.14
  68.2 22.7 %copy-start.16 = (f32[2,192,128]{2,1,0:T(8,128)}, f32[2,192,128]{2,1,0:T(8,128)S(1)}, u32[]{:S(2)}) copy-start(f32[2,192,128]{2,1,0:T(8,128)S(1)} %get-tuple-element.40.ws_ref) | copy-start | bytes 589828
  89.0 30.3 %collective-permute-start.5 = (bf16[16,96,256]{2,1,0:T(8,128)(2,1)S(1)}, bf16[16,96,256]{2,1,0:T(8,128)(2,1)S(1)}, u32[]{:S(2)}, u32[]{:S(2)}) collective-permute-start(bf16[16,96,256]{2,1,0:T(8,128)(2,1)S(1)} %all_to_all.25.own_ref), channel_id=1, source_target_pairs={{0,1},{1,0},{2,3},{3,2},{4,5},{5,4},{6,7},{7,6},{8,9},{9,8},{10,11... | collective-permute-start | bytes 2359304 | tf_op jit(solution)/shard_map/ppermute | solution.py:183
  90.9 47.4 %all-to-all-start.2 = ((bf16[16,96,256]{2,1,0:T(8,128)(2,1)}), bf16[16,96,256]{2,1,0:T(8,128)(2,1)S(1)}, u32[]{:S(2)}, u32[]{:S(2)}) async-start(bf16[16,96,256]{2,1,0:T(8,128)(2,1)} %get-tuple-element.30), calls=%async_computation.2 | async-start | bytes 1572864 | tf_op jit(solution)/shard_map/all_to_all | solution.py:191
  94.6 18.8 %collective-permute-start.6 = (bf16[3,172,256]{2,1,0:T(8,128)(2,1)S(1)}, bf16[3,172,256]{2,1,0:T(8,128)(2,1)S(1)}, u32[]{:S(2)}, u32[]{:S(2)}) collective-permute-start(bf16[3,172,256]{2,1,0:T(8,128)(2,1)S(1)} %collective-permute-done.f0), channel_id=1, source_target_pairs={{0,64},{64,128},{128,192},{192,0},{1,65},{65,129},{129,193},{193,1... | collective-permute-start | bytes 792584 | tf_op jit(solution)/shard_map/ppermute | solution.py:187
  98.5 20.8 %collective-permute-start.7 = (bf16[3,172,256]{2,1,0:T(8,128)(2,1)S(1)}, bf16[3,172,256]{2,1,0:T(8,128)(2,1)S(1)}, u32[]{:S(2)}, u32[]{:S(2)}) collective-permute-start(bf16[3,172,256]{2,1,0:T(8,128)(2,1)S(1)} %collective-permute-done.f0), channel_id=1, source_target_pairs={{0,128},{64,192},{128,0},{192,64},{1,129},{65,193},{129,1},{193,65... | collective-permute-start | bytes 792584 | tf_op jit(solution)/shard_map/ppermute | solution.py:187
  103.1 16.2 %collective-permute-start.8 = (bf16[3,172,256]{2,1,0:T(8,128)(2,1)S(1)}, bf16[3,172,256]{2,1,0:T(8,128)(2,1)S(1)}, u32[]{:S(2)}, u32[]{:S(2)}) collective-permute-start(bf16[3,172,256]{2,1,0:T(8,128)(2,1)S(1)} %collective-permute-done.f0), channel_id=1, source_target_pairs={{0,192},{64,0},{128,64},{192,128},{1,193},{65,1},{129,65},{193,129... | collective-permute-start | bytes 792584 | tf_op jit(solution)/shard_map/ppermute | solution.py:187
  119.3 0.9 copy-start.4
  120.1 1.1 copy-start.5
  121.3 1.0 copy-start.9
  122.2 1.0 copy-start.11
  123.2 1.0 copy-start.13
  124.1 1.0 copy-start.15
  125.1 0.9 copy-start.20
  126.0 0.9 copy-start.21
  126.9 0.9 copy-start.22
  132.8 1.2 copy-start
  134.0 0.9 copy-start.2
  134.9 0.8 copy-start.6
  135.7 0.7 copy-start.18
  136.4 4.5 %collective-permute-start.9 = (bf16[16,96,256]{2,1,0:T(8,128)(2,1)}, bf16[16,96,256]{2,1,0:T(8,128)(2,1)}, u32[]{:S(2)}, u32[]{:S(2)}) collective-permute-start(bf16[16,96,256]{2,1,0:T(8,128)(2,1)} %get-tuple-element.37), channel_id=1, source_target_pairs={{0,1},{1,0},{2,3},{3,2},{4,5},{5,4},{6,7},{7,6},{8,9},{9,8},{10,11... | collective-permute-start | bytes 2359304 | tf_op jit(solution)/shard_map/ppermute | solution.py:183
  138.3 4.3 %collective-permute-start.4 = (bf16[16,96,256]{2,1,0:T(8,128)(2,1)S(1)}, bf16[16,96,256]{2,1,0:T(8,128)(2,1)S(1)}, u32[]{:S(2)}, u32[]{:S(2)}) collective-permute-start(bf16[16,96,256]{2,1,0:T(8,128)(2,1)S(1)} %all-to-all-done.2.own_ref), channel_id=1, source_target_pairs={{0,1},{1,0},{2,3},{3,2},{4,5},{5,4},{6,7},{7,6},{8,9},{9,8},{10,11... | collective-permute-start | bytes 2359304 | tf_op jit(solution)/shard_map/ppermute | solution.py:183
  140.9 21.3 %copy-start.17 = (f32[2,192,128]{2,1,0:T(8,128)S(1)}, f32[2,192,128]{2,1,0:T(8,128)}, u32[]{:S(2)}) copy-start(f32[2,192,128]{2,1,0:T(8,128)} %copy-done.16) | copy-start | bytes 589828
  142.3 25.7 %copy-start.1 = (bf16[384,2048]{1,0:T(8,128)(2,1)S(1)}, bf16[384,2048]{1,0:T(8,128)(2,1)}, u32[]{:S(2)}) copy-start(bf16[384,2048]{1,0:T(8,128)(2,1)} %copy-done) | copy-start | bytes 4718596
  142.3 25.7 %copy-start.19 = (bf16[208,384]{1,0:T(8,128)(2,1)S(1)}, bf16[208,384]{1,0:T(8,128)(2,1)}, u32[]{:S(2)}) copy-start(bf16[208,384]{1,0:T(8,128)(2,1)} %copy-done.18) | copy-start | bytes 479236
  163.2 18.1 %all-to-all-start.4 = ((bf16[16,32,128]{2,1,0:T(8,128)(2,1)}), bf16[16,32,128]{2,1,0:T(8,128)(2,1)S(1)}, u32[]{:S(2)}, u32[]{:S(2)}) async-start(bf16[16,32,128]{2,1,0:T(8,128)(2,1)} %shard_map.132), calls=%async_computation.4 | async-start | bytes 262144 | tf_op jit(solution)/shard_map/all_to_all | solution.py:191
  168.0 1.2 copy-start.3
  169.2 1.1 copy-start.7

commit v3 on v2

--- a/solution.py
+++ b/solution.py
@@ -12,17 +12,64 @@
 ROWS = 2 * CAP
 NT = (((1,), (1,)), ((), ()))
 VM = pl.BlockSpec(memory_space=pltpu.VMEM)
+HB = pl.BlockSpec(memory_space=pltpu.HBM)
 SM = pl.BlockSpec(memory_space=pltpu.SMEM)
 
 
-def call(kernel, out_shape, in_specs, scratch=(), mib=8, flops=0):
+def call(body, out_shape, operands, scratch=(), mib=8, scalars=None, direct=None):
+    n, m = len(operands), len(out_shape)
+
+    def kernel(*refs):
+        refs = list(refs)
+        at = refs.pop(0) if scalars is not None else None
+        ins, outs, rest = refs[:n], refs[n : n + m], refs[n + m :]
+        in_bufs, out_bufs, rest = rest[:n], rest[n : n + m], rest[n + m :]
+        in_sem, out_sem, rest = rest[0], rest[1], rest[2:]
+        copies = {
+            i: pltpu.make_async_copy(ins[i], in_bufs[i], in_sem.at[i])
+            for i in range(n)
+            if i != direct
+        }
+        for copy in copies.values():
+            copy.start()
+
+        def get(i):
+            if i == direct:
+                return ins[i]
+            copies[i].wait()
+            return in_bufs[i]
+
+        written = []
+
+        def put(i):
+            copy = pltpu.make_async_copy(out_bufs[i], outs[i], out_sem.at[i])
+            copy.start()
+            written.append(copy)
+
+        body(at, get, out_bufs, put, *rest)
+        for copy in written:
+            copy.wait()
+
     return pl.pallas_call(
         kernel,
-        out_shape=out_shape,
-        in_specs=in_specs,
-        out_specs=jax.tree.map(lambda _: VM, out_shape),
-        scratch_shapes=scratch,
+        out_shape=tuple(pltpu.HBM(o.shape, o.dtype) for o in out_shape),
+        in_specs=([SM] if scalars is not None else [])
+        + [VM if i == direct else HB for i in range(n)],
+        out_specs=(HB,) * m,
+        scratch_shapes=[
+            pltpu.VMEM((8, 128) if i == direct else o.shape, o.dtype)
+            for i, o in enumerate(operands)
+        ]
+        + [pltpu.VMEM(o.shape, o.dtype) for o in out_shape]
+        + [pltpu.SemaphoreType.DMA((n,)), pltpu.SemaphoreType.DMA((m,))]
+        + list(scratch),
         compiler_params=pltpu.CompilerParams(vmem_limit_bytes=mib * 1024 * 1024),
+    )(
+        *(() if scalars is None else (scalars,)),
+        *[
+            o if i == direct else pltpu.with_memory_space_constraint(o, pltpu.HBM)
+            for i, o in enumerate(operands)
+        ],
     )
 
 
@@ -30,7 +77,9 @@
     return jax.ShapeDtypeStruct(shape, dtype)
 
 
-def pack_kernel(tok_ref, cot_ref, id_ref, w_ref, a_ref):
+def pack_kernel(at, get, outs, put):
+    (a_ref,) = outs
+    id_ref, w_ref, tok_ref, cot_ref = get(0), get(1), get(2), get(3)
     w = w_ref[...]
     high = w.astype(BF).astype(F32)
     mid = (w - high).astype(BF).astype(F32)
@@ -40,9 +89,12 @@
         a_ref[k, 0:32, :] = tok_ref[...]
         a_ref[k, 32:64, :] = cot_ref[...]
         a_ref[k, 64:72, :] = meta
-
-
-def select_kernel(at_ref, r_ref, tok_ref, cot_ref, back_ref, ws_ref):
+    put(0)
+
+
+def select_kernel(at_ref, get, outs, put):
+    tok_ref, cot_ref, back_ref, ws_ref = outs
+    r_ref = get(0)
     zh = at_ref[0]
     row8 = lax.broadcasted_iota(jnp.int32, (8, 128), 0)
     expert = jnp.where(row8 < NX, zh * NX + row8, -1).astype(F32)
@@ -80,6 +132,8 @@
             for x in range(NX):
                 for y in range(NY):
                     dst[x * NY + y, b * CAP : (b + 1) * CAP, :] = v[x * CAP : (x + 1) * CAP]
+    for i in range(4):
+        put(i)
 
 
 def spread(c):
@@ -107,32 +161,36 @@
 DENSE, NEW_AT, NEW = 172, 176, 20
 
 
-def forward_kernel(
-    at_ref, own_ref, oth_ref, n0, n1, n2, n3, f0, f1, f2, f3, ng_ref, nu_ref, nd_ref,
-    part_ref, away_ref, in_ref, gu_ref, hid_ref, down_ref, w_s,
-):
+def forward_kernel(at_ref, get, outs, put, w_s):
+    part_ref, away_ref, in_ref, gu_ref, hid_ref, down_ref = outs
     zh, c, at_x = at_ref[0], at_ref[1], at_ref[2]
     perm = spread(c)
-    join(own_ref, oth_ref, perm, in_ref)
+    join(get(0), get(1), perm, in_ref)
+    put(2)
+    ng_ref, nu_ref, nd_ref = get(10), get(11), get(12)
     for m, new in ((0, ng_ref), (1, nu_ref)):
         w_s[m, 160:HID, :] = jnp.zeros((HID - 160, 2048), BF)
         w_s[m, NEW_AT : NEW_AT + NEW, :] = new[...]
     down_ref[160:HID, :] = jnp.zeros((HID - 160, 2048), BF)
     down_ref[NEW_AT : NEW_AT + NEW, :] = nd_ref[...]
-    for half, refs in ((zh, (n0, n1, n2, n3)), (1 - zh, (f0, f1, f2, f3))):
-        for k, ref in enumerate(refs):
+    for first, half in ((2, zh), (6, 1 - zh)):
+        for k in range(NX):
+            ref = get(first + k)
             source = half * NX + ((at_x + NX - k) & (NX - 1))
             lanes = pl.ds(pl.multiple_of(source * 256, 256), 256)
             w_s[0, 0:DENSE, lanes] = ref[0]
             w_s[1, 0:DENSE, lanes] = ref[1]
             down_ref[0:DENSE, lanes] = ref[2]
+    put(5)
     gu = lax.dot_general(
         w_s[...].reshape(2 * HID, 2048), in_ref[...], NT, preferred_element_type=F32
     )
     gu_ref[...] = gu
+    put(3)
     gate, up = gu[0:HID], gu[HID : 2 * HID]
     hidden = gate * jax.nn.sigmoid(gate) * up
     hid_ref[...] = hidden.astype(BF)
+    put(4)
     rows = hidden.T.astype(BF)
     for y in range(NY):
         d = lax.dot_general(
@@ -142,12 +200,13 @@
         for x in range(NX):
             part_ref[x * NY + y] = o[x * ROWS : (x + 1) * ROWS, 0:256]
             away_ref[x * NY + y] = o[x * ROWS : (x + 1) * ROWS, 256:512].astype(BF)
-
-
-def grad_kernel(
-    at_ref, own_ref, oth_ref, in_ref, gu_ref, hid_ref, down_ref, gg_ref, gup_ref, gd_ref, sg_s
-):
-    join(own_ref, oth_ref, spread(at_ref[1]), sg_s)
+    put(1)
+    put(0)
+
+
+def grad_kernel(at_ref, get, outs, put, sg_s):
+    join(get(0), get(1), spread(at_ref[1]), sg_s)
+    in_ref, gu_ref, hid_ref, down_ref = get(2), get(3), get(4), get(5)
     sg = sg_s[...]
     inp = in_ref[...]
     gate, up = gu_ref[0:HID], gu_ref[HID : 2 * HID]
@@ -155,13 +214,17 @@
     gh = lax.dot_general(down_ref[...], sg, NT, preferred_element_type=F32)
     ggp = (gh * up * sig * (1.0 + gate * (1.0 - sig))).astype(BF)
     gup = (gh * (gate * sig)).astype(BF)
-    for lhs, rhs, out in ((ggp, inp, gg_ref), (gup, inp, gup_ref), (hid_ref[...], sg, gd_ref)):
+    for i, (lhs, rhs) in enumerate(((hid_ref[...], sg), (ggp, inp), (gup, inp))):
+        out = outs[i]
         g = jnp.dot(lhs, rhs, preferred_element_type=F32).astype(BF)
         out[0:DENSE, :] = g[0:DENSE]
         out[DENSE : DENSE + NEW, :] = g[NEW_AT : NEW_AT + NEW]
-
-
-def combine_kernel(r_ref, back_ref, ws_ref, send_ref):
+        put(i)
+
+
+def combine_kernel(at, get, outs, put):
+    (send_ref,) = outs
+    r_ref, back_ref, ws_ref = get(0), get(1), get(2)
     sums = []
     for x in range(NX):
         s = r_ref[x * NY].astype(F32)
@@ -177,6 +240,7 @@
             back_ref[b], lo, preferred_element_type=F32
         )
         send_ref[b * ZL : (b + 1) * ZL] = m.T.astype(BF).reshape(ZL, 32, 128)
+    put(0)
 
 
 def swap(v, axis):
@@ -209,24 +273,32 @@
 
     mine = jnp.stack([dense_gate.T, dense_up.T, dense_down])
     theirs = swap(mine, "zh")
-    payload = call(pack_kernel, sds((16, 72, 128), BF), [VM] * 4)(
-        tokens.T, cotangent.T, expert_ids.T, route_weights.T
+    mine, tokens = lax.optimization_barrier((mine, tokens))
+    (payload,) = call(
+        pack_kernel,
+        [sds((16, 72, 128), BF)],
+        [expert_ids.T, route_weights.T, tokens.T, cotangent.T],
     )
     near = [mine] + [turn(mine, k) for k in range(1, NX)]
     got = exchange(payload, Z)
-    got, theirs, near = lax.optimization_barrier((got, theirs, near))
+    got, theirs = lax.optimization_barrier((got, theirs))
     tok_send, cot_send, back, ws = call(
         select_kernel,
-        (
+        [
             sds((16, ROWS, 256), BF),
             sds((16, ROWS, 256), BF),
             sds((ZH, 128, NX * CAP), BF),
             sds((ZH, NX * CAP, 128), F32),
-        ),
-        [SM, VM],
-    )(at, got)
+        ],
+        [got],
+        scalars=at,
+        direct=0,
+    )
+    tok_send, near = lax.optimization_barrier((tok_send, near))
     own = exchange(tok_send, XY)
     far = [theirs] + [turn(theirs, k) for k in range(1, NX)]
+    oth = swap(own, "c")
+    own, far = lax.optimization_barrier((own, far))
     oth = swap(own, "c")
     cot_send, _ = lax.optimization_barrier((cot_send, own))
     own_cot = exchange(cot_send, XY)
@@ -234,29 +306,32 @@
 
     part, away, inp, gu, hidden, down = call(
         forward_kernel,
-        (
+        [
             sds((16, ROWS, 256), F32),
             sds((16, ROWS, 256), BF),
             sds((NX * ROWS, 2048), BF),
             sds((2 * HID, NX * ROWS), F32),
             sds((HID, NX * ROWS), BF),
             sds((HID, 2048), BF),
-        ),
-        [SM] + [VM] * 13,
+        ],
+        [own, oth, *near, *far, noise_gate[0].T, noise_up[0].T, noise_down[0]],
         [pltpu.VMEM((2, HID, 2048), BF)],
-        mib=28,
-    )(at, own, oth, *near, *far, noise_gate[0].T, noise_up[0].T, noise_down[0])
+        mib=32,
+        scalars=at,
+        direct=1,
+    )
     send = (part + swap(away, "c").astype(F32)).astype(BF)
     own_cot, oth_cot, send = lax.optimization_barrier((own_cot, oth_cot, send))
-    gg, gup, gd = call(
+    gd, gg, gup = call(
         grad_kernel,
-        (sds((hid, 2048), BF),) * 3,
-        [SM] + [VM] * 6,
+        [sds((hid, 2048), BF)] * 3,
+        [own_cot, oth_cot, inp, gu, hidden, down],
         [pltpu.VMEM((NX * ROWS, 2048), BF)],
-        mib=28,
-    )(at, own_cot, oth_cot, inp, gu, hidden, down)
+        mib=32,
+        scalars=at,
+    )
     got = exchange(send, XY)
-    send = call(combine_kernel, sds((16, 32, 128), BF), [VM] * 3)(got, back, ws)
+    (send,) = call(combine_kernel, [sds((16, 32, 128), BF)], [got, back, ws], direct=0)
     got = exchange(send, Z)
     mixed = jnp.sum(got.astype(F32), axis=0).astype(BF).T
     return mixed, gg[None], gup[None], gd[None]

time: 183 us -> 163 us (0.89)
  blocking collectives: 40.3 us -> 17.8 us
  local copies, waits for them, and re-layouts: 18.5 us -> 1.52 us
  starting transfers between devices: 64.2 us -> 71.3 us
  waiting for transfers between devices: 41.7 us -> 48.3 us
  Pallas kernels: 13.3 us -> 19.2 us
    all_to_all x2 -> x1, blocking collectives: 40.3 us -> 17.8 us  [exchange(): return lax.all_to_all(v, axes, 0, 0, tiled=True)]
    unnamed x54 -> x22, local copies, waits for them, and re-layouts: 18.5 us -> 1.52 us
    all_to_all x3 -> x4, starting transfers between devices: 23.7 us -> 31.1 us  [exchange(): return lax.all_to_all(v, axes, 0, 0, tiled=True)]
    all_to_all x3 -> x4, waiting for transfers between devices: 6.68 us -> 13.1 us  [exchange(): return lax.all_to_all(v, axes, 0, 0, tiled=True)]
    pallas_call x5, Pallas kernels: 13.3 us -> 19.2 us  [call(): pl.pallas_call(kernel, out_shape=tuple((pltpu.HBM(o.shape, o.dtype) for o...]
  transfers between devices with their start and end apart: 13 -> 14, of which waited for: 6 -> 6; matrix products, arithmetic and copies ran while one was open for 1% -> 1% of each run, Pallas kernels for 5% -> 9%
where the time goes in v3:
time: 163 us; the launch traced here: 162 us
  starting transfers between devices  71.3 us (44%)
  waiting for transfers between devices  48.3 us (30%)
  Pallas kernels  19.2 us (12%)
  blocking collectives  17.8 us (11%)
  other arithmetic  3.36 us (2%)
    all_to_all x4, starting transfers between devices, exchange(): return lax.all_to_all(v, axes, 0, 0, tiled=True)  31.1 us
    ppermute x4, waiting for transfers between devices, swap(): return lax.ppermute(v, axis, [(0, 1), (1, 0)])  23.3 us
    ppermute x6, starting transfers between devices, turn(): return lax.ppermute(v, 'x', [(i, (i + k) % NX) for i in range(NX)])  23.2 us
    pallas_call x5, Pallas kernels, call(): pl.pallas_call(kernel, out_shape=tuple((pltpu.HBM(o.shape, o.dtype) for o...  19.2 us
    all_to_all x1, blocking collectives, exchange(): return lax.all_to_all(v, axes, 0, 0, tiled=True)  17.8 us
    ppermute x4, starting transfers between devices, swap(): return lax.ppermute(v, axis, [(0, 1), (1, 0)])  17.1 us
    all_to_all x4, waiting for transfers between devices, exchange(): return lax.all_to_all(v, axes, 0, 0, tiled=True)  13.1 us
    ppermute x6, waiting for transfers between devices, turn(): return lax.ppermute(v, 'x', [(i, (i + k) % NX) for i in range(NX)])  11.9 us
  transfers between devices with their start and end apart: 14, of which 6 were waited for; matrix products, arithmetic and copies ran while one was open for 1% of the time, Pallas kernels for 9%

profile of v3, /device:TPU:32, one launch (start us, length us, event | category | flops | bytes accessed | tf_op | source)
XLA Modules:
  0.0 162.4 jit_solution(15032081915610651337)
XLA Ops:
  0.6 1.0 pad_maximum_fusion.refs_3_
  1.6 0.0 copy-start.2
  1.7 1.6 %shard_map.129 = bf16[16,72,128]{2,1,0:T(8,128)(2,1)} custom-call(s32[2,128]{1,0:T(2,128)} %bitcast.34, f32[2,128]{1,0:T(2,128)} %bitcast.35, bf16[32,128]{1,0:T(8,128)(2,1)} %bitcast.31, bf16[32,128]{1,0:T(8,128)(2,1)} %bitcast.32), custom_call_target="tpu_custom_call" | custom-call | tf_op jit(solution)/shard_map/pallas_call | solution.py:53
  3.3 15.2 %all-to-all-start = ((bf16[16,72,128]{2,1,0:T(8,128)(2,1)}), bf16[16,72,128]{2,1,0:T(8,128)(2,1)S(1)}, u32[]{:S(2)}, u32[]{:S(2)}) async-start(bf16[16,72,128]{2,1,0:T(8,128)(2,1)} %shard_map.129), calls=%async_computation | async-start | bytes 589824 | tf_op jit(solution)/shard_map/all_to_all | solution.py:255
  18.5 11.2 %collective-permute-start = (bf16[3,172,256]{2,1,0:T(8,128)(2,1)S(1)}, bf16[3,172,256]{2,1,0:T(8,128)(2,1)S(1)}, u32[]{:S(2)}, u32[]{:S(2)}) collective-permute-start(bf16[3,172,256]{2,1,0:T(8,128)(2,1)S(1)} %pad_maximum_fusion.refs_3_), channel_id=1, source_target_pairs={{0,256},{256,0},{1,257},{257,1},{2,258},{258,2},{3,259},{259,3},{4... | collective-permute-start | bytes 792584 | tf_op jit(solution)/shard_map/ppermute | solution.py:247
  29.7 3.4 %collective-permute-start.1 = (bf16[3,172,256]{2,1,0:T(8,128)(2,1)S(1)}, bf16[3,172,256]{2,1,0:T(8,128)(2,1)S(1)}, u32[]{:S(2)}, u32[]{:S(2)}) collective-permute-start(bf16[3,172,256]{2,1,0:T(8,128)(2,1)S(1)} %pad_maximum_fusion.refs_3_), channel_id=1, source_target_pairs={{0,64},{64,128},{128,192},{192,0},{1,65},{65,129},{129,193},{193,1... | collective-permute-start | bytes 792584 | tf_op jit(solution)/shard_map/ppermute | solution.py:251
  33.1 4.6 %collective-permute-start.2 = (bf16[3,172,256]{2,1,0:T(8,128)(2,1)S(1)}, bf16[3,172,256]{2,1,0:T(8,128)(2,1)S(1)}, u32[]{:S(2)}, u32[]{:S(2)}) collective-permute-start(bf16[3,172,256]{2,1,0:T(8,128)(2,1)S(1)} %pad_maximum_fusion.refs_3_), channel_id=1, source_target_pairs={{0,128},{64,192},{128,0},{192,64},{1,129},{65,193},{129,1},{193,65... | collective-permute-start | bytes 792584 | tf_op jit(solution)/shard_map/ppermute | solution.py:251
  37.8 3.3 %collective-permute-start.3 = (bf16[3,172,256]{2,1,0:T(8,128)(2,1)S(1)}, bf16[3,172,256]{2,1,0:T(8,128)(2,1)S(1)}, u32[]{:S(2)}, u32[]{:S(2)}) collective-permute-start(bf16[3,172,256]{2,1,0:T(8,128)(2,1)S(1)} %pad_maximum_fusion.refs_3_), channel_id=1, source_target_pairs={{0,192},{64,0},{128,64},{192,128},{1,193},{65,1},{129,65},{193,129... | collective-permute-start | bytes 792584 | tf_op jit(solution)/shard_map/ppermute | solution.py:251
  41.1 0.1 pad_add_fusion.refs_0_
  41.2 22.7 %collective-permute-done.refs_7_ = bf16[3,172,256]{2,1,0:T(8,128)(2,1)S(1)} collective-permute-done((bf16[3,172,256]{2,1,0:T(8,128)(2,1)S(1)}, bf16[3,172,256]{2,1,0:T(8,128)(2,1)S(1)}, u32[]{:S(2)}, u32[]{:S(2)}) %collective-permute-start) | collective-permute-done | bytes 264224 | tf_op jit(solution)/shard_map/ppermute | solution.py:247
  63.9 0.0 copy-start.4
  64.0 0.0 all-to-all-done.refs_1_
  64.0 2.3 %shard_map.130 = (bf16[16,96,256]{2,1,0:T(8,128)(2,1)}, bf16[16,96,256]{2,1,0:T(8,128)(2,1)}, bf16[2,128,192]{2,1,0:T(8,128)(2,1)}, f32[2,192,128]{2,1,0:T(8,128)}) custom-call(s32[3]{0:T(128)S(1)} %pad_add_fusion.refs_0_, bf16[16,72,128]{2,1,0:T(8,128)(2,1)S(1)} %all-to-all-done.refs_1_), custom_call_target="tpu_custom_call" | custom-call | tf_op jit(solution)/shard_map/pallas_call | solution.py:53
  66.3 0.0 collective-permute-done.1.refs_4_
  66.3 0.0 copy-start.5
  66.3 0.0 collective-permute-done.2.refs_5_
  66.3 0.0 copy-start.6
  66.3 0.0 collective-permute-done.3.refs_6_
  66.4 0.0 copy-start.7
  66.4 0.8 copy-done.7
  67.1 7.0 %all-to-all-start.1 = ((bf16[16,96,256]{2,1,0:T(8,128)(2,1)}), bf16[16,96,256]{2,1,0:T(8,128)(2,1)S(1)}, u32[]{:S(2)}, u32[]{:S(2)}) async-start(bf16[16,96,256]{2,1,0:T(8,128)(2,1)} %get-tuple-element.40), calls=%async_computation.1 | async-start | bytes 1572864 | tf_op jit(solution)/shard_map/all_to_all | solution.py:255
  74.2 3.8 %collective-permute-start.4 = (bf16[3,172,256]{2,1,0:T(8,128)(2,1)S(1)}, bf16[3,172,256]{2,1,0:T(8,128)(2,1)S(1)}, u32[]{:S(2)}, u32[]{:S(2)}) collective-permute-start(bf16[3,172,256]{2,1,0:T(8,128)(2,1)S(1)} %collective-permute-done.refs_7_), channel_id=1, source_target_pairs={{0,64},{64,128},{128,192},{192,0},{1,65},{65,129},{129,193},{193,1... | collective-permute-start | bytes 792584 | tf_op jit(solution)/shard_map/ppermute | solution.py:251
  78.0 4.6 %collective-permute-start.5 = (bf16[3,172,256]{2,1,0:T(8,128)(2,1)S(1)}, bf16[3,172,256]{2,1,0:T(8,128)(2,1)S(1)}, u32[]{:S(2)}, u32[]{:S(2)}) collective-permute-start(bf16[3,172,256]{2,1,0:T(8,128)(2,1)S(1)} %collective-permute-done.refs_7_), channel_id=1, source_target_pairs={{0,128},{64,192},{128,0},{192,64},{1,129},{65,193},{129,1},{193,65... | collective-permute-start | bytes 792584 | tf_op jit(solution)/shard_map/ppermute | solution.py:251
  82.6 3.4 %collective-permute-start.6 = (bf16[3,172,256]{2,1,0:T(8,128)(2,1)S(1)}, bf16[3,172,256]{2,1,0:T(8,128)(2,1)S(1)}, u32[]{:S(2)}, u32[]{:S(2)}) collective-permute-start(bf16[3,172,256]{2,1,0:T(8,128)(2,1)S(1)} %collective-permute-done.refs_7_), channel_id=1, source_target_pairs={{0,192},{64,0},{128,64},{192,128},{1,193},{65,1},{129,65},{193,129... | collective-permute-start | bytes 792584 | tf_op jit(solution)/shard_map/ppermute | solution.py:251
  86.0 7.0 %collective-permute-done.4.refs_8_ = bf16[3,172,256]{2,1,0:T(8,128)(2,1)S(1)} collective-permute-done((bf16[3,172,256]{2,1,0:T(8,128)(2,1)S(1)}, bf16[3,172,256]{2,1,0:T(8,128)(2,1)S(1)}, u32[]{:S(2)}, u32[]{:S(2)}) %collective-permute-start.4) | collective-permute-done | bytes 264224 | tf_op jit(solution)/shard_map/ppermute | solution.py:251
  93.0 0.0 copy-start.8
  93.0 4.8 %collective-permute-done.5.refs_9_ = bf16[3,172,256]{2,1,0:T(8,128)(2,1)S(1)} collective-permute-done((bf16[3,172,256]{2,1,0:T(8,128)(2,1)S(1)}, bf16[3,172,256]{2,1,0:T(8,128)(2,1)S(1)}, u32[]{:S(2)}, u32[]{:S(2)}) %collective-permute-start.5) | collective-permute-done | bytes 264224 | tf_op jit(solution)/shard_map/ppermute | solution.py:251
  97.8 0.0 copy-start.9
  97.8 0.0 collective-permute-done.6.refs_10_
  97.8 0.0 copy-start.10
  97.8 0.7 copy-done.10
  98.5 0.0 all-to-all-done.1.refs_1_
  98.6 0.0 copy-start
  98.6 1.9 %collective-permute-start.8 = (bf16[16,96,256]{2,1,0:T(8,128)(2,1)S(1)}, bf16[16,96,256]{2,1,0:T(8,128)(2,1)S(1)}, u32[]{:S(2)}, u32[]{:S(2)}) collective-permute-start(bf16[16,96,256]{2,1,0:T(8,128)(2,1)S(1)} %all-to-all-done.1.refs_1_), channel_id=1, source_target_pairs={{0,1},{1,0},{2,3},{3,2},{4,5},{5,4},{6,7},{7,6},{8,9},{9,8},{10,11... | collective-permute-start | bytes 2359304 | tf_op jit(solution)/shard_map/ppermute | solution.py:247
  100.5 0.0 copy-done.8
  100.5 0.0 copy-done.9
  100.5 0.0 copy-done.2
  100.5 0.0 copy-done.4
  100.5 0.0 copy-done.5
  100.5 0.0 copy-done.6
  100.5 5.0 %all-to-all-start.2 = ((bf16[16,96,256]{2,1,0:T(8,128)(2,1)}), bf16[16,96,256]{2,1,0:T(8,128)(2,1)S(1)}, u32[]{:S(2)}, u32[]{:S(2)}) async-start(bf16[16,96,256]{2,1,0:T(8,128)(2,1)} %get-tuple-element.43), calls=%async_computation.2 | async-start | bytes 1572864 | tf_op jit(solution)/shard_map/all_to_all | solution.py:255
  105.6 0.0 collective-permute-done.8.refs_2_
  105.6 0.0 copy-done
  105.6 7.1 %shard_map.131 = (f32[16,96,256]{2,1,0:T(8,128)}, bf16[16,96,256]{2,1,0:T(8,128)(2,1)}, bf16[384,2048]{1,0:T(8,128)(2,1)}, f32[416,384]{1,0:T(8,128)}, bf16[208,...) custom-call(s32[3]{0:T(128)S(1)} %pad_add_fusion.refs_0_, bf16[16,96,256]{2,1,0:T(8,128)(2,1)} %copy-done, ...), custom_call_target="tpu_custom_call" | custom-call | tf_op jit(solution)/shard_map/pallas_call | solution.py:53
  112.7 2.1 %collective-permute-start.9 = (bf16[16,96,256]{2,1,0:T(8,128)(2,1)}, bf16[16,96,256]{2,1,0:T(8,128)(2,1)S(1)}, u32[]{:S(2)}, u32[]{:S(2)}) collective-permute-start(bf16[16,96,256]{2,1,0:T(8,128)(2,1)} %get-tuple-element.53), channel_id=1, source_target_pairs={{0,1},{1,0},{2,3},{3,2},{4,5},{5,4},{6,7},{7,6},{8,9},{9,8},{10,11... | collective-permute-start | bytes 2359304 | tf_op jit(solution)/shard_map/ppermute | solution.py:247
  114.8 6.1 %all-to-all-done.2.refs_1_ = bf16[16,96,256]{2,1,0:T(8,128)(2,1)S(1)} async-done(((bf16[16,96,256]{2,1,0:T(8,128)(2,1)}), bf16[16,96,256]{2,1,0:T(8,128)(2,1)S(1)}, u32[]{:S(2)}, u32[]{:S(2)}) %all-to-all-start.2) | async-done | bytes 786464 | tf_op jit(solution)/shard_map/all_to_all | solution.py:255
  120.8 0.0 copy-start.1
  120.8 1.9 %collective-permute-start.7 = (bf16[16,96,256]{2,1,0:T(8,128)(2,1)S(1)}, bf16[16,96,256]{2,1,0:T(8,128)(2,1)S(1)}, u32[]{:S(2)}, u32[]{:S(2)}) collective-permute-start(bf16[16,96,256]{2,1,0:T(8,128)(2,1)S(1)} %all-to-all-done.2.refs_1_), channel_id=1, source_target_pairs={{0,1},{1,0},{2,3},{3,2},{4,5},{5,4},{6,7},{7,6},{8,9},{9,8},{10,11... | collective-permute-start | bytes 2359304 | tf_op jit(solution)/shard_map/ppermute | solution.py:247
  122.8 0.0 collective-permute-done.9
  122.8 1.6 %add_convert_fusion = bf16[16,96,256]{2,1,0:T(8,128)(2,1)S(1)} fusion(f32[16,96,256]{2,1,0:T(8,128)} %get-tuple-element.52, bf16[16,96,256]{2,1,0:T(8,128)(2,1)S(1)} %collective-permute-done.9), kind=kLoop, calls=%fused_computation | loop fusion | flops 1179648 | bytes 3145728 | tf_op jit(solution)/shard_map/convert_element_type | solution.py:323
  124.4 0.0 copy-done.1
  124.4 0.6 collective-permute-done.7.refs_2_
  125.0 0.0 copy-start.3
  125.0 17.8 %all_to_all.25.refs_0_ = bf16[16,96,256]{2,1,0:T(8,128)(2,1)S(1)} all-to-all(bf16[16,96,256]{2,1,0:T(8,128)(2,1)S(1)} %add_convert_fusion), channel_id=1, replica_groups=mesh['zh'=2,'x'=4,'y'=4,'zl'=8,'c'=2] {'x','y'}, dimensions={0} | all-to-all | bytes 1572864 | tf_op jit(solution)/shard_map/all_to_all | solution.py:255
  142.8 2.1 %shard_map.132 = bf16[16,32,128]{2,1,0:T(8,128)(2,1)} custom-call(bf16[16,96,256]{2,1,0:T(8,128)(2,1)S(1)} %all_to_all.25.refs_0_, bf16[2,128,192]{2,1,0:T(8,128)(2,1)} %get-tuple-element.55.refs_1_, f32[2,192,128]{2,1,0:T(8,128)} %get-tuple-element.56.refs_2_), custom_call_target="tpu_custom_call" | custom-call | tf_op jit(solution)/shard_map/pallas_call | solution.py:53
  144.9 3.8 %all-to-all-start.4 = ((bf16[16,32,128]{2,1,0:T(8,128)(2,1)}), bf16[16,32,128]{2,1,0:T(8,128)(2,1)S(1)}, u32[]{:S(2)}, u32[]{:S(2)}) async-start(bf16[16,32,128]{2,1,0:T(8,128)(2,1)} %shard_map.132), calls=%async_computation.4 | async-start | bytes 262144 | tf_op jit(solution)/shard_map/all_to_all | solution.py:255
  148.7 0.0 copy-done.3
  148.7 6.0 %shard_map.133 = (bf16[192,2048]{1,0:T(8,128)(2,1)}, bf16[192,2048]{1,0:T(8,128)(2,1)}, bf16[192,2048]{1,0:T(8,128)(2,1)}) custom-call(s32[3]{0:T(128)S(1)} %pad_add_fusion.refs_0_, bf16[16,96,256]{2,1,0:T(8,128)(2,1)} %copy-done.1, bf16[16,96,256]{2,1,0:T(8,128)(2,1)} %copy-done.3, bf16[384,2048]{1,0:T(8,128)(2,1)} %get-tuple-element.59.refs_3_, ...), custom_call_target="tpu_custom_call" | custom-call | tf_op jit(solution)/shard_map/pallas_call | solution.py:53
  154.7 7.1 %all-to-all-done.4 = bf16[16,32,128]{2,1,0:T(8,128)(2,1)S(1)} async-done(((bf16[16,32,128]{2,1,0:T(8,128)(2,1)}), bf16[16,32,128]{2,1,0:T(8,128)(2,1)S(1)}, u32[]{:S(2)}, u32[]{:S(2)}) %all-to-all-start.4) | async-done | bytes 131104 | tf_op jit(solution)/shard_map/all_to_all | solution.py:255
  161.8 0.6 reduce_sum.12
Async XLA Ops:
  1.6 98.8 %copy-start.2 = (bf16[3,172,256]{2,1,0:T(8,128)(2,1)}, bf16[3,172,256]{2,1,0:T(8,128)(2,1)S(1)}, u32[]{:S(2)}) copy-start(bf16[3,172,256]{2,1,0:T(8,128)(2,1)S(1)} %pad_maximum_fusion.refs_3_) | copy-start | bytes 792580
  3.3 60.6 %all-to-all-start = ((bf16[16,72,128]{2,1,0:T(8,128)(2,1)}), bf16[16,72,128]{2,1,0:T(8,128)(2,1)S(1)}, u32[]{:S(2)}, u32[]{:S(2)}) async-start(bf16[16,72,128]{2,1,0:T(8,128)(2,1)} %shard_map.129), calls=%async_computation | async-start | bytes 589824 | tf_op jit(solution)/shard_map/all_to_all | solution.py:255
  18.5 45.4 %collective-permute-start = (bf16[3,172,256]{2,1,0:T(8,128)(2,1)S(1)}, bf16[3,172,256]{2,1,0:T(8,128)(2,1)S(1)}, u32[]{:S(2)}, u32[]{:S(2)}) collective-permute-start(bf16[3,172,256]{2,1,0:T(8,128)(2,1)S(1)} %pad_maximum_fusion.refs_3_), channel_id=1, source_target_pairs={{0,256},{256,0},{1,257},{257,1},{2,258},{258,2},{3,259},{259,3},{4... | collective-permute-start | bytes 792584 | tf_op jit(solution)/shard_map/ppermute | solution.py:247
  29.7 36.6 %collective-permute-start.1 = (bf16[3,172,256]{2,1,0:T(8,128)(2,1)S(1)}, bf16[3,172,256]{2,1,0:T(8,128)(2,1)S(1)}, u32[]{:S(2)}, u32[]{:S(2)}) collective-permute-start(bf16[3,172,256]{2,1,0:T(8,128)(2,1)S(1)} %pad_maximum_fusion.refs_3_), channel_id=1, source_target_pairs={{0,64},{64,128},{128,192},{192,0},{1,65},{65,129},{129,193},{193,1... | collective-permute-start | bytes 792584 | tf_op jit(solution)/shard_map/ppermute | solution.py:251
  33.1 33.2 %collective-permute-start.2 = (bf16[3,172,256]{2,1,0:T(8,128)(2,1)S(1)}, bf16[3,172,256]{2,1,0:T(8,128)(2,1)S(1)}, u32[]{:S(2)}, u32[]{:S(2)}) collective-permute-start(bf16[3,172,256]{2,1,0:T(8,128)(2,1)S(1)} %pad_maximum_fusion.refs_3_), channel_id=1, source_target_pairs={{0,128},{64,192},{128,0},{192,64},{1,129},{65,193},{129,1},{193,65... | collective-permute-start | bytes 792584 | tf_op jit(solution)/shard_map/ppermute | solution.py:251
  37.8 28.6 %collective-permute-start.3 = (bf16[3,172,256]{2,1,0:T(8,128)(2,1)S(1)}, bf16[3,172,256]{2,1,0:T(8,128)(2,1)S(1)}, u32[]{:S(2)}, u32[]{:S(2)}) collective-permute-start(bf16[3,172,256]{2,1,0:T(8,128)(2,1)S(1)} %pad_maximum_fusion.refs_3_), channel_id=1, source_target_pairs={{0,192},{64,0},{128,64},{192,128},{1,193},{65,1},{129,65},{193,129... | collective-permute-start | bytes 792584 | tf_op jit(solution)/shard_map/ppermute | solution.py:251
  63.9 36.6 %copy-start.4 = (bf16[3,172,256]{2,1,0:T(8,128)(2,1)}, bf16[3,172,256]{2,1,0:T(8,128)(2,1)S(1)}, u32[]{:S(2)}) copy-start(bf16[3,172,256]{2,1,0:T(8,128)(2,1)S(1)} %collective-permute-done.refs_7_) | copy-start | bytes 792580
  66.3 34.2 %copy-start.5 = (bf16[3,172,256]{2,1,0:T(8,128)(2,1)}, bf16[3,172,256]{2,1,0:T(8,128)(2,1)S(1)}, u32[]{:S(2)}) copy-start(bf16[3,172,256]{2,1,0:T(8,128)(2,1)S(1)} %collective-permute-done.1.refs_4_) | copy-start | bytes 792580
  66.3 34.2 %copy-start.6 = (bf16[3,172,256]{2,1,0:T(8,128)(2,1)}, bf16[3,172,256]{2,1,0:T(8,128)(2,1)S(1)}, u32[]{:S(2)}) copy-start(bf16[3,172,256]{2,1,0:T(8,128)(2,1)S(1)} %collective-permute-done.2.refs_5_) | copy-start | bytes 792580
  66.4 0.8 copy-start.7
  67.1 31.4 %all-to-all-start.1 = ((bf16[16,96,256]{2,1,0:T(8,128)(2,1)}), bf16[16,96,256]{2,1,0:T(8,128)(2,1)S(1)}, u32[]{:S(2)}, u32[]{:S(2)}) async-start(bf16[16,96,256]{2,1,0:T(8,128)(2,1)} %get-tuple-element.40), calls=%async_computation.1 | async-start | bytes 1572864 | tf_op jit(solution)/shard_map/all_to_all | solution.py:255
  74.2 18.8 %collective-permute-start.4 = (bf16[3,172,256]{2,1,0:T(8,128)(2,1)S(1)}, bf16[3,172,256]{2,1,0:T(8,128)(2,1)S(1)}, u32[]{:S(2)}, u32[]{:S(2)}) collective-permute-start(bf16[3,172,256]{2,1,0:T(8,128)(2,1)S(1)} %collective-permute-done.refs_7_), channel_id=1, source_target_pairs={{0,64},{64,128},{128,192},{192,0},{1,65},{65,129},{129,193},{193,1... | collective-permute-start | bytes 792584 | tf_op jit(solution)/shard_map/ppermute | solution.py:251
  78.0 19.8 %collective-permute-start.5 = (bf16[3,172,256]{2,1,0:T(8,128)(2,1)S(1)}, bf16[3,172,256]{2,1,0:T(8,128)(2,1)S(1)}, u32[]{:S(2)}, u32[]{:S(2)}) collective-permute-start(bf16[3,172,256]{2,1,0:T(8,128)(2,1)S(1)} %collective-permute-done.refs_7_), channel_id=1, source_target_pairs={{0,128},{64,192},{128,0},{192,64},{1,129},{65,193},{129,1},{193,65... | collective-permute-start | bytes 792584 | tf_op jit(solution)/shard_map/ppermute | solution.py:251
  82.6 15.2 %collective-permute-start.6 = (bf16[3,172,256]{2,1,0:T(8,128)(2,1)S(1)}, bf16[3,172,256]{2,1,0:T(8,128)(2,1)S(1)}, u32[]{:S(2)}, u32[]{:S(2)}) collective-permute-start(bf16[3,172,256]{2,1,0:T(8,128)(2,1)S(1)} %collective-permute-done.refs_7_), channel_id=1, source_target_pairs={{0,192},{64,0},{128,64},{192,128},{1,193},{65,1},{129,65},{193,129... | collective-permute-start | bytes 792584 | tf_op jit(solution)/shard_map/ppermute | solution.py:251
  93.0 7.5 %copy-start.8 = (bf16[3,172,256]{2,1,0:T(8,128)(2,1)}, bf16[3,172,256]{2,1,0:T(8,128)(2,1)S(1)}, u32[]{:S(2)}) copy-start(bf16[3,172,256]{2,1,0:T(8,128)(2,1)S(1)} %collective-permute-done.4.refs_8_) | copy-start | bytes 792580
  97.8 2.7 %copy-start.9 = (bf16[3,172,256]{2,1,0:T(8,128)(2,1)}, bf16[3,172,256]{2,1,0:T(8,128)(2,1)S(1)}, u32[]{:S(2)}) copy-start(bf16[3,172,256]{2,1,0:T(8,128)(2,1)S(1)} %collective-permute-done.5.refs_9_) | copy-start | bytes 792580
  97.8 0.7 copy-start.10
  98.6 7.0 %copy-start = (bf16[16,96,256]{2,1,0:T(8,128)(2,1)}, bf16[16,96,256]{2,1,0:T(8,128)(2,1)S(1)}, u32[]{:S(2)}) copy-start(bf16[16,96,256]{2,1,0:T(8,128)(2,1)S(1)} %all-to-all-done.1.refs_1_) | copy-start | bytes 2359300
  98.6 7.0 %collective-permute-start.8 = (bf16[16,96,256]{2,1,0:T(8,128)(2,1)S(1)}, bf16[16,96,256]{2,1,0:T(8,128)(2,1)S(1)}, u32[]{:S(2)}, u32[]{:S(2)}) collective-permute-start(bf16[16,96,256]{2,1,0:T(8,128)(2,1)S(1)} %all-to-all-done.1.refs_1_), channel_id=1, source_target_pairs={{0,1},{1,0},{2,3},{3,2},{4,5},{5,4},{6,7},{7,6},{8,9},{9,8},{10,11... | collective-permute-start | bytes 2359304 | tf_op jit(solution)/shard_map/ppermute | solution.py:247
  100.5 20.3 %all-to-all-start.2 = ((bf16[16,96,256]{2,1,0:T(8,128)(2,1)}), bf16[16,96,256]{2,1,0:T(8,128)(2,1)S(1)}, u32[]{:S(2)}, u32[]{:S(2)}) async-start(bf16[16,96,256]{2,1,0:T(8,128)(2,1)} %get-tuple-element.43), calls=%async_computation.2 | async-start | bytes 1572864 | tf_op jit(solution)/shard_map/all_to_all | solution.py:255
  112.7 10.1 %collective-permute-start.9 = (bf16[16,96,256]{2,1,0:T(8,128)(2,1)}, bf16[16,96,256]{2,1,0:T(8,128)(2,1)S(1)}, u32[]{:S(2)}, u32[]{:S(2)}) collective-permute-start(bf16[16,96,256]{2,1,0:T(8,128)(2,1)} %get-tuple-element.53), channel_id=1, source_target_pairs={{0,1},{1,0},{2,3},{3,2},{4,5},{5,4},{6,7},{7,6},{8,9},{9,8},{10,11... | collective-permute-start | bytes 2359304 | tf_op jit(solution)/shard_map/ppermute | solution.py:247
  120.8 3.6 %copy-start.1 = (bf16[16,96,256]{2,1,0:T(8,128)(2,1)}, bf16[16,96,256]{2,1,0:T(8,128)(2,1)S(1)}, u32[]{:S(2)}) copy-start(bf16[16,96,256]{2,1,0:T(8,128)(2,1)S(1)} %all-to-all-done.2.refs_1_) | copy-start | bytes 2359300
  120.8 4.2 %collective-permute-start.7 = (bf16[16,96,256]{2,1,0:T(8,128)(2,1)S(1)}, bf16[16,96,256]{2,1,0:T(8,128)(2,1)S(1)}, u32[]{:S(2)}, u32[]{:S(2)}) collective-permute-start(bf16[16,96,256]{2,1,0:T(8,128)(2,1)S(1)} %all-to-all-done.2.refs_1_), channel_id=1, source_target_pairs={{0,1},{1,0},{2,3},{3,2},{4,5},{5,4},{6,7},{7,6},{8,9},{9,8},{10,11... | collective-permute-start | bytes 2359304 | tf_op jit(solution)/shard_map/ppermute | solution.py:247
  125.0 23.7 %copy-start.3 = (bf16[16,96,256]{2,1,0:T(8,128)(2,1)}, bf16[16,96,256]{2,1,0:T(8,128)(2,1)S(1)}, u32[]{:S(2)}) copy-start(bf16[16,96,256]{2,1,0:T(8,128)(2,1)S(1)} %collective-permute-done.7.refs_2_) | copy-start | bytes 2359300
  144.9 16.9 %all-to-all-start.4 = ((bf16[16,32,128]{2,1,0:T(8,128)(2,1)}), bf16[16,32,128]{2,1,0:T(8,128)(2,1)S(1)}, u32[]{:S(2)}, u32[]{:S(2)}) async-start(bf16[16,32,128]{2,1,0:T(8,128)(2,1)} %shard_map.132), calls=%async_computation.4 | async-start | bytes 262144 | tf_op jit(solution)/shard_map/all_to_all | solution.py:255

commit v4 on v3

--- a/solution.py
+++ b/solution.py
@@ -273,7 +273,6 @@
 
     mine = jnp.stack([dense_gate.T, dense_up.T, dense_down])
     theirs = swap(mine, "zh")
-    mine, tokens = lax.optimization_barrier((mine, tokens))
     (payload,) = call(
         pack_kernel,
         [sds((16, 72, 128), BF)],
@@ -296,9 +295,11 @@
     )
     tok_send, near = lax.optimization_barrier((tok_send, near))
     own = exchange(tok_send, XY)
-    far = [theirs] + [turn(theirs, k) for k in range(1, NX)]
+    two, one, three = turn(theirs, 2), turn(theirs, 1), turn(theirs, 3)
+    far = [theirs, one, two, three]
     oth = swap(own, "c")
-    own, far = lax.optimization_barrier((own, far))
+    own, two, one, three = lax.optimization_barrier((own, two, one, three))
+    far = [theirs, one, two, three]
     oth = swap(own, "c")
     cot_send, _ = lax.optimization_barrier((cot_send, own))
     own_cot = exchange(cot_send, XY)

time: 163 us -> 163 us (level)
  starting transfers between devices: 71.3 us -> 73.3 us
  waiting for transfers between devices: 48.3 us -> 46.3 us
  transfers between devices with their start and end apart: 14 -> 14, of which waited for: 6 -> 6; matrix products, arithmetic and copies ran while one was open for 1% -> 2% of each run, Pallas kernels for 9% -> 9%
where the time goes in v4:
time: 163 us; the launch traced here: 162 us
  starting transfers between devices  73.3 us (45%)
  waiting for transfers between devices  46.3 us (28%)
  Pallas kernels  19 us (12%)
  blocking collectives  17.8 us (11%)
  other arithmetic  3.35 us (2%)
    all_to_all x4, starting transfers between devices, exchange(): return lax.all_to_all(v, axes, 0, 0, tiled=True)  32.4 us
    ppermute x6, starting transfers between devices, turn(): return lax.ppermute(v, 'x', [(i, (i + k) % NX) for i in range(NX)])  23.8 us
    ppermute x4, waiting for transfers between devices, swap(): return lax.ppermute(v, axis, [(0, 1), (1, 0)])  22.3 us
    pallas_call x5, Pallas kernels, call(): pl.pallas_call(kernel, out_shape=tuple((pltpu.HBM(o.shape, o.dtype) for o...  19 us
    all_to_all x1, blocking collectives, exchange(): return lax.all_to_all(v, axes, 0, 0, tiled=True)  17.8 us
    ppermute x4, starting transfers between devices, swap(): return lax.ppermute(v, axis, [(0, 1), (1, 0)])  17.1 us
    all_to_all x4, waiting for transfers between devices, exchange(): return lax.all_to_all(v, axes, 0, 0, tiled=True)  13.1 us
    ppermute x6, waiting for transfers between devices, turn(): return lax.ppermute(v, 'x', [(i, (i + k) % NX) for i in range(NX)])  10.9 us
  transfers between devices with their start and end apart: 14, of which 6 were waited for; matrix products, arithmetic and copies ran while one was open for 2% of the time, Pallas kernels for 9%

profile of v4, /device:TPU:32, one launch (start us, length us, event | category | flops | bytes accessed | tf_op | source)
XLA Modules:
  0.0 162.3 jit_solution(10827702367227120779)
XLA Ops:
  0.6 1.5 shard_map.129
  2.2 15.2 %all-to-all-start = ((bf16[16,72,128]{2,1,0:T(8,128)(2,1)}), bf16[16,72,128]{2,1,0:T(8,128)(2,1)S(1)}, u32[]{:S(2)}, u32[]{:S(2)}) async-start(bf16[16,72,128]{2,1,0:T(8,128)(2,1)} %shard_map.129), calls=%async_computation | async-start | bytes 589824 | tf_op jit(solution)/shard_map/all_to_all | solution.py:255
  17.4 1.0 pad_maximum_fusion.refs_3_
  18.4 0.0 copy-start.2
  18.4 11.2 %collective-permute-start = (bf16[3,172,256]{2,1,0:T(8,128)(2,1)S(1)}, bf16[3,172,256]{2,1,0:T(8,128)(2,1)S(1)}, u32[]{:S(2)}, u32[]{:S(2)}) collective-permute-start(bf16[3,172,256]{2,1,0:T(8,128)(2,1)S(1)} %pad_maximum_fusion.refs_3_), channel_id=1, source_target_pairs={{0,256},{256,0},{1,257},{257,1},{2,258},{258,2},{3,259},{259,3},{4... | collective-permute-start | bytes 792584 | tf_op jit(solution)/shard_map/ppermute | solution.py:247
  29.6 3.4 %collective-permute-start.1 = (bf16[3,172,256]{2,1,0:T(8,128)(2,1)S(1)}, bf16[3,172,256]{2,1,0:T(8,128)(2,1)S(1)}, u32[]{:S(2)}, u32[]{:S(2)}) collective-permute-start(bf16[3,172,256]{2,1,0:T(8,128)(2,1)S(1)} %pad_maximum_fusion.refs_3_), channel_id=1, source_target_pairs={{0,64},{64,128},{128,192},{192,0},{1,65},{65,129},{129,193},{193,1... | collective-permute-start | bytes 792584 | tf_op jit(solution)/shard_map/ppermute | solution.py:251
  33.0 4.6 %collective-permute-start.2 = (bf16[3,172,256]{2,1,0:T(8,128)(2,1)S(1)}, bf16[3,172,256]{2,1,0:T(8,128)(2,1)S(1)}, u32[]{:S(2)}, u32[]{:S(2)}) collective-permute-start(bf16[3,172,256]{2,1,0:T(8,128)(2,1)S(1)} %pad_maximum_fusion.refs_3_), channel_id=1, source_target_pairs={{0,128},{64,192},{128,0},{192,64},{1,129},{65,193},{129,1},{193,65... | collective-permute-start | bytes 792584 | tf_op jit(solution)/shard_map/ppermute | solution.py:251
  37.7 3.3 %collective-permute-start.3 = (bf16[3,172,256]{2,1,0:T(8,128)(2,1)S(1)}, bf16[3,172,256]{2,1,0:T(8,128)(2,1)S(1)}, u32[]{:S(2)}, u32[]{:S(2)}) collective-permute-start(bf16[3,172,256]{2,1,0:T(8,128)(2,1)S(1)} %pad_maximum_fusion.refs_3_), channel_id=1, source_target_pairs={{0,192},{64,0},{128,64},{192,128},{1,193},{65,1},{129,65},{193,129... | collective-permute-start | bytes 792584 | tf_op jit(solution)/shard_map/ppermute | solution.py:251
  41.0 0.1 pad_add_fusion.refs_0_
  41.1 21.7 %collective-permute-done.refs_7_ = bf16[3,172,256]{2,1,0:T(8,128)(2,1)S(1)} collective-permute-done((bf16[3,172,256]{2,1,0:T(8,128)(2,1)S(1)}, bf16[3,172,256]{2,1,0:T(8,128)(2,1)S(1)}, u32[]{:S(2)}, u32[]{:S(2)}) %collective-permute-start) | collective-permute-done | bytes 264224 | tf_op jit(solution)/shard_map/ppermute | solution.py:247
  62.8 0.0 copy-start.4
  62.8 0.0 all-to-all-done.refs_1_
  62.8 2.3 %shard_map.130 = (bf16[16,96,256]{2,1,0:T(8,128)(2,1)}, bf16[16,96,256]{2,1,0:T(8,128)(2,1)}, bf16[2,128,192]{2,1,0:T(8,128)(2,1)}, f32[2,192,128]{2,1,0:T(8,128)}) custom-call(s32[3]{0:T(128)S(1)} %pad_add_fusion.refs_0_, bf16[16,72,128]{2,1,0:T(8,128)(2,1)S(1)} %all-to-all-done.refs_1_), custom_call_target="tpu_custom_call" | custom-call | tf_op jit(solution)/shard_map/pallas_call | solution.py:53
  65.2 0.0 collective-permute-done.1.refs_4_
  65.2 0.0 copy-start.5
  65.2 0.0 collective-permute-done.2.refs_5_
  65.2 0.0 copy-start.6
  65.2 0.0 collective-permute-done.3.refs_6_
  65.2 0.0 copy-start.7
  65.2 0.8 copy-done.7
  66.0 7.0 %all-to-all-start.1 = ((bf16[16,96,256]{2,1,0:T(8,128)(2,1)}), bf16[16,96,256]{2,1,0:T(8,128)(2,1)S(1)}, u32[]{:S(2)}, u32[]{:S(2)}) async-start(bf16[16,96,256]{2,1,0:T(8,128)(2,1)} %get-tuple-element.35), calls=%async_computation.1 | async-start | bytes 1572864 | tf_op jit(solution)/shard_map/all_to_all | solution.py:255
  73.0 5.3 %collective-permute-start.4 = (bf16[3,172,256]{2,1,0:T(8,128)(2,1)S(1)}, bf16[3,172,256]{2,1,0:T(8,128)(2,1)S(1)}, u32[]{:S(2)}, u32[]{:S(2)}) collective-permute-start(bf16[3,172,256]{2,1,0:T(8,128)(2,1)S(1)} %collective-permute-done.refs_7_), channel_id=1, source_target_pairs={{0,128},{64,192},{128,0},{192,64},{1,129},{65,193},{129,1},{193,65... | collective-permute-start | bytes 792584 | tf_op jit(solution)/shard_map/ppermute | solution.py:251
  78.4 2.5 %collective-permute-start.5 = (bf16[3,172,256]{2,1,0:T(8,128)(2,1)S(1)}, bf16[3,172,256]{2,1,0:T(8,128)(2,1)S(1)}, u32[]{:S(2)}, u32[]{:S(2)}) collective-permute-start(bf16[3,172,256]{2,1,0:T(8,128)(2,1)S(1)} %collective-permute-done.refs_7_), channel_id=1, source_target_pairs={{0,64},{64,128},{128,192},{192,0},{1,65},{65,129},{129,193},{193,1... | collective-permute-start | bytes 792584 | tf_op jit(solution)/shard_map/ppermute | solution.py:251
  80.9 4.6 %collective-permute-start.6 = (bf16[3,172,256]{2,1,0:T(8,128)(2,1)S(1)}, bf16[3,172,256]{2,1,0:T(8,128)(2,1)S(1)}, u32[]{:S(2)}, u32[]{:S(2)}) collective-permute-start(bf16[3,172,256]{2,1,0:T(8,128)(2,1)S(1)} %collective-permute-done.refs_7_), channel_id=1, source_target_pairs={{0,192},{64,0},{128,64},{192,128},{1,193},{65,1},{129,65},{193,129... | collective-permute-start | bytes 792584 | tf_op jit(solution)/shard_map/ppermute | solution.py:251
  85.5 7.1 %collective-permute-done.4.refs_9_ = bf16[3,172,256]{2,1,0:T(8,128)(2,1)S(1)} collective-permute-done((bf16[3,172,256]{2,1,0:T(8,128)(2,1)S(1)}, bf16[3,172,256]{2,1,0:T(8,128)(2,1)S(1)}, u32[]{:S(2)}, u32[]{:S(2)}) %collective-permute-start.4) | collective-permute-done | bytes 264224 | tf_op jit(solution)/shard_map/ppermute | solution.py:251
  92.5 0.0 copy-start.8
  92.6 3.8 %collective-permute-done.5.refs_8_ = bf16[3,172,256]{2,1,0:T(8,128)(2,1)S(1)} collective-permute-done((bf16[3,172,256]{2,1,0:T(8,128)(2,1)S(1)}, bf16[3,172,256]{2,1,0:T(8,128)(2,1)S(1)}, u32[]{:S(2)}, u32[]{:S(2)}) %collective-permute-start.5) | collective-permute-done | bytes 264224 | tf_op jit(solution)/shard_map/ppermute | solution.py:251
  96.4 0.0 copy-start.9
  96.4 0.0 collective-permute-done.6.refs_10_
  96.4 0.0 copy-start.10
  96.4 0.7 copy-done.10
  97.1 0.0 all-to-all-done.1.refs_1_
  97.1 0.0 copy-start
  97.1 1.9 %collective-permute-start.8 = (bf16[16,96,256]{2,1,0:T(8,128)(2,1)S(1)}, bf16[16,96,256]{2,1,0:T(8,128)(2,1)S(1)}, u32[]{:S(2)}, u32[]{:S(2)}) collective-permute-start(bf16[16,96,256]{2,1,0:T(8,128)(2,1)S(1)} %all-to-all-done.1.refs_1_), channel_id=1, source_target_pairs={{0,1},{1,0},{2,3},{3,2},{4,5},{5,4},{6,7},{7,6},{8,9},{9,8},{10,11... | collective-permute-start | bytes 2359304 | tf_op jit(solution)/shard_map/ppermute | solution.py:247
  99.0 0.0 copy-done.8
  99.0 0.0 copy-done.9
  99.0 0.0 copy-done.2
  99.0 0.0 copy-done.4
  99.0 0.0 copy-done.5
  99.1 0.0 copy-done.6
  99.1 5.4 %all-to-all-start.2 = ((bf16[16,96,256]{2,1,0:T(8,128)(2,1)}), bf16[16,96,256]{2,1,0:T(8,128)(2,1)S(1)}, u32[]{:S(2)}, u32[]{:S(2)}) async-start(bf16[16,96,256]{2,1,0:T(8,128)(2,1)} %get-tuple-element.38), calls=%async_computation.2 | async-start | bytes 1572864 | tf_op jit(solution)/shard_map/all_to_all | solution.py:255
  104.4 0.0 collective-permute-done.8.refs_2_
  104.4 0.0 copy-done
  104.5 7.1 %shard_map.131 = (f32[16,96,256]{2,1,0:T(8,128)}, bf16[16,96,256]{2,1,0:T(8,128)(2,1)}, bf16[384,2048]{1,0:T(8,128)(2,1)}, f32[416,384]{1,0:T(8,128)}, bf16[208,...) custom-call(s32[3]{0:T(128)S(1)} %pad_add_fusion.refs_0_, bf16[16,96,256]{2,1,0:T(8,128)(2,1)} %copy-done, ...), custom_call_target="tpu_custom_call" | custom-call | tf_op jit(solution)/shard_map/pallas_call | solution.py:53
  111.5 2.1 %collective-permute-start.9 = (bf16[16,96,256]{2,1,0:T(8,128)(2,1)}, bf16[16,96,256]{2,1,0:T(8,128)(2,1)S(1)}, u32[]{:S(2)}, u32[]{:S(2)}) collective-permute-start(bf16[16,96,256]{2,1,0:T(8,128)(2,1)} %get-tuple-element.47), channel_id=1, source_target_pairs={{0,1},{1,0},{2,3},{3,2},{4,5},{5,4},{6,7},{7,6},{8,9},{9,8},{10,11... | collective-permute-start | bytes 2359304 | tf_op jit(solution)/shard_map/ppermute | solution.py:247
  113.7 6.1 %all-to-all-done.2.refs_1_ = bf16[16,96,256]{2,1,0:T(8,128)(2,1)S(1)} async-done(((bf16[16,96,256]{2,1,0:T(8,128)(2,1)}), bf16[16,96,256]{2,1,0:T(8,128)(2,1)S(1)}, u32[]{:S(2)}, u32[]{:S(2)}) %all-to-all-start.2) | async-done | bytes 786464 | tf_op jit(solution)/shard_map/all_to_all | solution.py:255
  119.7 0.0 copy-start.1
  119.7 1.9 %collective-permute-start.7 = (bf16[16,96,256]{2,1,0:T(8,128)(2,1)S(1)}, bf16[16,96,256]{2,1,0:T(8,128)(2,1)S(1)}, u32[]{:S(2)}, u32[]{:S(2)}) collective-permute-start(bf16[16,96,256]{2,1,0:T(8,128)(2,1)S(1)} %all-to-all-done.2.refs_1_), channel_id=1, source_target_pairs={{0,1},{1,0},{2,3},{3,2},{4,5},{5,4},{6,7},{7,6},{8,9},{9,8},{10,11... | collective-permute-start | bytes 2359304 | tf_op jit(solution)/shard_map/ppermute | solution.py:247
  121.6 0.0 collective-permute-done.9
  121.6 1.6 %add_convert_fusion = bf16[16,96,256]{2,1,0:T(8,128)(2,1)S(1)} fusion(f32[16,96,256]{2,1,0:T(8,128)} %get-tuple-element.46, bf16[16,96,256]{2,1,0:T(8,128)(2,1)S(1)} %collective-permute-done.9), kind=kLoop, calls=%fused_computation | loop fusion | flops 1179648 | bytes 3145728 | tf_op jit(solution)/shard_map/convert_element_type | solution.py:324
  123.3 0.0 copy-done.1
  123.3 0.6 collective-permute-done.7.refs_2_
  123.9 0.0 copy-start.3
  123.9 17.8 %all_to_all.25.refs_0_ = bf16[16,96,256]{2,1,0:T(8,128)(2,1)S(1)} all-to-all(bf16[16,96,256]{2,1,0:T(8,128)(2,1)S(1)} %add_convert_fusion), channel_id=1, replica_groups=mesh['zh'=2,'x'=4,'y'=4,'zl'=8,'c'=2] {'x','y'}, dimensions={0} | all-to-all | bytes 1572864 | tf_op jit(solution)/shard_map/all_to_all | solution.py:255
  141.7 2.1 %shard_map.132 = bf16[16,32,128]{2,1,0:T(8,128)(2,1)} custom-call(bf16[16,96,256]{2,1,0:T(8,128)(2,1)S(1)} %all_to_all.25.refs_0_, bf16[2,128,192]{2,1,0:T(8,128)(2,1)} %get-tuple-element.49.refs_1_, f32[2,192,128]{2,1,0:T(8,128)} %get-tuple-element.50.refs_2_), custom_call_target="tpu_custom_call" | custom-call | tf_op jit(solution)/shard_map/pallas_call | solution.py:53
  143.8 4.8 %all-to-all-start.4 = ((bf16[16,32,128]{2,1,0:T(8,128)(2,1)}), bf16[16,32,128]{2,1,0:T(8,128)(2,1)S(1)}, u32[]{:S(2)}, u32[]{:S(2)}) async-start(bf16[16,32,128]{2,1,0:T(8,128)(2,1)} %shard_map.132), calls=%async_computation.4 | async-start | bytes 262144 | tf_op jit(solution)/shard_map/all_to_all | solution.py:255
  148.5 0.0 copy-done.3
  148.6 6.0 %shard_map.133 = (bf16[192,2048]{1,0:T(8,128)(2,1)}, bf16[192,2048]{1,0:T(8,128)(2,1)}, bf16[192,2048]{1,0:T(8,128)(2,1)}) custom-call(s32[3]{0:T(128)S(1)} %pad_add_fusion.refs_0_, bf16[16,96,256]{2,1,0:T(8,128)(2,1)} %copy-done.1, bf16[16,96,256]{2,1,0:T(8,128)(2,1)} %copy-done.3, bf16[384,2048]{1,0:T(8,128)(2,1)} %get-tuple-element.53.refs_3_, ...), custom_call_target="tpu_custom_call" | custom-call | tf_op jit(solution)/shard_map/pallas_call | solution.py:53
  154.6 7.1 %all-to-all-done.4 = bf16[16,32,128]{2,1,0:T(8,128)(2,1)S(1)} async-done(((bf16[16,32,128]{2,1,0:T(8,128)(2,1)}), bf16[16,32,128]{2,1,0:T(8,128)(2,1)S(1)}, u32[]{:S(2)}, u32[]{:S(2)}) %all-to-all-start.4) | async-done | bytes 131104 | tf_op jit(solution)/shard_map/all_to_all | solution.py:255
  161.6 0.6 reduce_sum.12
Async XLA Ops:
  2.2 60.6 %all-to-all-start = ((bf16[16,72,128]{2,1,0:T(8,128)(2,1)}), bf16[16,72,128]{2,1,0:T(8,128)(2,1)S(1)}, u32[]{:S(2)}, u32[]{:S(2)}) async-start(bf16[16,72,128]{2,1,0:T(8,128)(2,1)} %shard_map.129), calls=%async_computation | async-start | bytes 589824 | tf_op jit(solution)/shard_map/all_to_all | solution.py:255
  18.4 80.6 %copy-start.2 = (bf16[3,172,256]{2,1,0:T(8,128)(2,1)}, bf16[3,172,256]{2,1,0:T(8,128)(2,1)S(1)}, u32[]{:S(2)}) copy-start(bf16[3,172,256]{2,1,0:T(8,128)(2,1)S(1)} %pad_maximum_fusion.refs_3_) | copy-start | bytes 792580
  18.4 44.4 %collective-permute-start = (bf16[3,172,256]{2,1,0:T(8,128)(2,1)S(1)}, bf16[3,172,256]{2,1,0:T(8,128)(2,1)S(1)}, u32[]{:S(2)}, u32[]{:S(2)}) collective-permute-start(bf16[3,172,256]{2,1,0:T(8,128)(2,1)S(1)} %pad_maximum_fusion.refs_3_), channel_id=1, source_target_pairs={{0,256},{256,0},{1,257},{257,1},{2,258},{258,2},{3,259},{259,3},{4... | collective-permute-start | bytes 792584 | tf_op jit(solution)/shard_map/ppermute | solution.py:247
  29.6 35.6 %collective-permute-start.1 = (bf16[3,172,256]{2,1,0:T(8,128)(2,1)S(1)}, bf16[3,172,256]{2,1,0:T(8,128)(2,1)S(1)}, u32[]{:S(2)}, u32[]{:S(2)}) collective-permute-start(bf16[3,172,256]{2,1,0:T(8,128)(2,1)S(1)} %pad_maximum_fusion.refs_3_), channel_id=1, source_target_pairs={{0,64},{64,128},{128,192},{192,0},{1,65},{65,129},{129,193},{193,1... | collective-permute-start | bytes 792584 | tf_op jit(solution)/shard_map/ppermute | solution.py:251
  33.0 32.2 %collective-permute-start.2 = (bf16[3,172,256]{2,1,0:T(8,128)(2,1)S(1)}, bf16[3,172,256]{2,1,0:T(8,128)(2,1)S(1)}, u32[]{:S(2)}, u32[]{:S(2)}) collective-permute-start(bf16[3,172,256]{2,1,0:T(8,128)(2,1)S(1)} %pad_maximum_fusion.refs_3_), channel_id=1, source_target_pairs={{0,128},{64,192},{128,0},{192,64},{1,129},{65,193},{129,1},{193,65... | collective-permute-start | bytes 792584 | tf_op jit(solution)/shard_map/ppermute | solution.py:251
  37.7 27.6 %collective-permute-start.3 = (bf16[3,172,256]{2,1,0:T(8,128)(2,1)S(1)}, bf16[3,172,256]{2,1,0:T(8,128)(2,1)S(1)}, u32[]{:S(2)}, u32[]{:S(2)}) collective-permute-start(bf16[3,172,256]{2,1,0:T(8,128)(2,1)S(1)} %pad_maximum_fusion.refs_3_), channel_id=1, source_target_pairs={{0,192},{64,0},{128,64},{192,128},{1,193},{65,1},{129,65},{193,129... | collective-permute-start | bytes 792584 | tf_op jit(solution)/shard_map/ppermute | solution.py:251
  62.8 36.2 %copy-start.4 = (bf16[3,172,256]{2,1,0:T(8,128)(2,1)}, bf16[3,172,256]{2,1,0:T(8,128)(2,1)S(1)}, u32[]{:S(2)}) copy-start(bf16[3,172,256]{2,1,0:T(8,128)(2,1)S(1)} %collective-permute-done.refs_7_) | copy-start | bytes 792580
  65.2 33.9 %copy-start.5 = (bf16[3,172,256]{2,1,0:T(8,128)(2,1)}, bf16[3,172,256]{2,1,0:T(8,128)(2,1)S(1)}, u32[]{:S(2)}) copy-start(bf16[3,172,256]{2,1,0:T(8,128)(2,1)S(1)} %collective-permute-done.1.refs_4_) | copy-start | bytes 792580
  65.2 33.8 %copy-start.6 = (bf16[3,172,256]{2,1,0:T(8,128)(2,1)}, bf16[3,172,256]{2,1,0:T(8,128)(2,1)S(1)}, u32[]{:S(2)}) copy-start(bf16[3,172,256]{2,1,0:T(8,128)(2,1)S(1)} %collective-permute-done.2.refs_5_) | copy-start | bytes 792580
  65.2 0.8 copy-start.7
  66.0 31.1 %all-to-all-start.1 = ((bf16[16,96,256]{2,1,0:T(8,128)(2,1)}), bf16[16,96,256]{2,1,0:T(8,128)(2,1)S(1)}, u32[]{:S(2)}, u32[]{:S(2)}) async-start(bf16[16,96,256]{2,1,0:T(8,128)(2,1)} %get-tuple-element.35), calls=%async_computation.1 | async-start | bytes 1572864 | tf_op jit(solution)/shard_map/all_to_all | solution.py:255
  73.0 19.5 %collective-permute-start.4 = (bf16[3,172,256]{2,1,0:T(8,128)(2,1)S(1)}, bf16[3,172,256]{2,1,0:T(8,128)(2,1)S(1)}, u32[]{:S(2)}, u32[]{:S(2)}) collective-permute-start(bf16[3,172,256]{2,1,0:T(8,128)(2,1)S(1)} %collective-permute-done.refs_7_), channel_id=1, source_target_pairs={{0,128},{64,192},{128,0},{192,64},{1,129},{65,193},{129,1},{193,65... | collective-permute-start | bytes 792584 | tf_op jit(solution)/shard_map/ppermute | solution.py:251
  78.4 18.0 %collective-permute-start.5 = (bf16[3,172,256]{2,1,0:T(8,128)(2,1)S(1)}, bf16[3,172,256]{2,1,0:T(8,128)(2,1)S(1)}, u32[]{:S(2)}, u32[]{:S(2)}) collective-permute-start(bf16[3,172,256]{2,1,0:T(8,128)(2,1)S(1)} %collective-permute-done.refs_7_), channel_id=1, source_target_pairs={{0,64},{64,128},{128,192},{192,0},{1,65},{65,129},{129,193},{193,1... | collective-permute-start | bytes 792584 | tf_op jit(solution)/shard_map/ppermute | solution.py:251
  80.9 15.5 %collective-permute-start.6 = (bf16[3,172,256]{2,1,0:T(8,128)(2,1)S(1)}, bf16[3,172,256]{2,1,0:T(8,128)(2,1)S(1)}, u32[]{:S(2)}, u32[]{:S(2)}) collective-permute-start(bf16[3,172,256]{2,1,0:T(8,128)(2,1)S(1)} %collective-permute-done.refs_7_), channel_id=1, source_target_pairs={{0,192},{64,0},{128,64},{192,128},{1,193},{65,1},{129,65},{193,129... | collective-permute-start | bytes 792584 | tf_op jit(solution)/shard_map/ppermute | solution.py:251
  92.5 6.5 %copy-start.8 = (bf16[3,172,256]{2,1,0:T(8,128)(2,1)}, bf16[3,172,256]{2,1,0:T(8,128)(2,1)S(1)}, u32[]{:S(2)}) copy-start(bf16[3,172,256]{2,1,0:T(8,128)(2,1)S(1)} %collective-permute-done.4.refs_9_) | copy-start | bytes 792580
  96.4 2.7 %copy-start.9 = (bf16[3,172,256]{2,1,0:T(8,128)(2,1)}, bf16[3,172,256]{2,1,0:T(8,128)(2,1)S(1)}, u32[]{:S(2)}) copy-start(bf16[3,172,256]{2,1,0:T(8,128)(2,1)S(1)} %collective-permute-done.5.refs_8_) | copy-start | bytes 792580
  96.4 0.7 copy-start.10
  97.1 7.4 %copy-start = (bf16[16,96,256]{2,1,0:T(8,128)(2,1)}, bf16[16,96,256]{2,1,0:T(8,128)(2,1)S(1)}, u32[]{:S(2)}) copy-start(bf16[16,96,256]{2,1,0:T(8,128)(2,1)S(1)} %all-to-all-done.1.refs_1_) | copy-start | bytes 2359300
  97.1 7.4 %collective-permute-start.8 = (bf16[16,96,256]{2,1,0:T(8,128)(2,1)S(1)}, bf16[16,96,256]{2,1,0:T(8,128)(2,1)S(1)}, u32[]{:S(2)}, u32[]{:S(2)}) collective-permute-start(bf16[16,96,256]{2,1,0:T(8,128)(2,1)S(1)} %all-to-all-done.1.refs_1_), channel_id=1, source_target_pairs={{0,1},{1,0},{2,3},{3,2},{4,5},{5,4},{6,7},{7,6},{8,9},{9,8},{10,11... | collective-permute-start | bytes 2359304 | tf_op jit(solution)/shard_map/ppermute | solution.py:247
  99.1 20.7 %all-to-all-start.2 = ((bf16[16,96,256]{2,1,0:T(8,128)(2,1)}), bf16[16,96,256]{2,1,0:T(8,128)(2,1)S(1)}, u32[]{:S(2)}, u32[]{:S(2)}) async-start(bf16[16,96,256]{2,1,0:T(8,128)(2,1)} %get-tuple-element.38), calls=%async_computation.2 | async-start | bytes 1572864 | tf_op jit(solution)/shard_map/all_to_all | solution.py:255
  111.5 10.1 %collective-permute-start.9 = (bf16[16,96,256]{2,1,0:T(8,128)(2,1)}, bf16[16,96,256]{2,1,0:T(8,128)(2,1)S(1)}, u32[]{:S(2)}, u32[]{:S(2)}) collective-permute-start(bf16[16,96,256]{2,1,0:T(8,128)(2,1)} %get-tuple-element.47), channel_id=1, source_target_pairs={{0,1},{1,0},{2,3},{3,2},{4,5},{5,4},{6,7},{7,6},{8,9},{9,8},{10,11... | collective-permute-start | bytes 2359304 | tf_op jit(solution)/shard_map/ppermute | solution.py:247
  119.7 3.6 %copy-start.1 = (bf16[16,96,256]{2,1,0:T(8,128)(2,1)}, bf16[16,96,256]{2,1,0:T(8,128)(2,1)S(1)}, u32[]{:S(2)}) copy-start(bf16[16,96,256]{2,1,0:T(8,128)(2,1)S(1)} %all-to-all-done.2.refs_1_) | copy-start | bytes 2359300
  119.7 4.2 %collective-permute-start.7 = (bf16[16,96,256]{2,1,0:T(8,128)(2,1)S(1)}, bf16[16,96,256]{2,1,0:T(8,128)(2,1)S(1)}, u32[]{:S(2)}, u32[]{:S(2)}) collective-permute-start(bf16[16,96,256]{2,1,0:T(8,128)(2,1)S(1)} %all-to-all-done.2.refs_1_), channel_id=1, source_target_pairs={{0,1},{1,0},{2,3},{3,2},{4,5},{5,4},{6,7},{7,6},{8,9},{9,8},{10,11... | collective-permute-start | bytes 2359304 | tf_op jit(solution)/shard_map/ppermute | solution.py:247
  123.9 24.7 %copy-start.3 = (bf16[16,96,256]{2,1,0:T(8,128)(2,1)}, bf16[16,96,256]{2,1,0:T(8,128)(2,1)S(1)}, u32[]{:S(2)}) copy-start(bf16[16,96,256]{2,1,0:T(8,128)(2,1)S(1)} %collective-permute-done.7.refs_2_) | copy-start | bytes 2359300
  143.8 17.9 %all-to-all-start.4 = ((bf16[16,32,128]{2,1,0:T(8,128)(2,1)}), bf16[16,32,128]{2,1,0:T(8,128)(2,1)S(1)}, u32[]{:S(2)}, u32[]{:S(2)}) async-start(bf16[16,32,128]{2,1,0:T(8,128)(2,1)} %shard_map.132), calls=%async_computation.4 | async-start | bytes 262144 | tf_op jit(solution)/shard_map/all_to_all | solution.py:255

commit v5 on v4

--- a/solution.py
+++ b/solution.py
@@ -85,10 +85,9 @@
     mid = (w - high).astype(BF).astype(F32)
     low = w - high - mid
     meta = jnp.concatenate([id_ref[...].astype(F32), high, mid, low], axis=0).astype(BF)
-    for k in range(ZH * ZL):
-        a_ref[k, 0:32, :] = tok_ref[...]
-        a_ref[k, 32:64, :] = cot_ref[...]
-        a_ref[k, 64:72, :] = meta
+    a_ref[0:32, :] = tok_ref[...]
+    a_ref[32:64, :] = cot_ref[...]
+    a_ref[64:72, :] = meta
     put(0)
 
 
@@ -275,11 +274,11 @@
     theirs = swap(mine, "zh")
     (payload,) = call(
         pack_kernel,
-        [sds((16, 72, 128), BF)],
+        [sds((72, 128), BF)],
         [expert_ids.T, route_weights.T, tokens.T, cotangent.T],
     )
     near = [mine] + [turn(mine, k) for k in range(1, NX)]
-    got = exchange(payload, Z)
+    got = lax.all_gather(payload, Z, axis=0, tiled=False)
     got, theirs = lax.optimization_barrier((got, theirs))
     tok_send, cot_send, back, ws = call(
         select_kernel,

time: 163 us -> 163 us (level)
  blocking collectives: 17.8 us -> 52.8 us
  waiting for transfers between devices: 46.3 us -> 18.4 us
  starting transfers between devices: 73.3 us -> 65.9 us
    all_gather x0 -> x1, blocking collectives: none -> 35 us  [local(): got = lax.all_gather(payload, Z, axis=0, tiled=False)]
    ppermute x4, waiting for transfers between devices: 22.3 us -> 0.58 us  [swap(): return lax.ppermute(v, axis, [(0, 1), (1, 0)])]
    all_to_all x4 -> x3, starting transfers between devices: 32.4 us -> 21.3 us  [exchange(): return lax.all_to_all(v, axes, 0, 0, tiled=True)]
    ppermute x6, waiting for transfers between devices: 10.9 us -> 5.02 us  [turn(): return lax.ppermute(v, 'x', [(i, (i + k) % NX) for i in range(NX)])]
    ppermute x4, starting transfers between devices: 17.1 us -> 20.8 us  [swap(): return lax.ppermute(v, axis, [(0, 1), (1, 0)])]
    all_to_all x4 -> x3, waiting for transfers between devices: 13.1 us -> 12.8 us  [exchange(): return lax.all_to_all(v, axes, 0, 0, tiled=True)]
  transfers between devices with their start and end apart: 14 -> 13, of which waited for: 6 -> 5; matrix products, arithmetic and copies ran while one was open for 2% -> 1% of each run, Pallas kernels for 9% -> 10%
where the time goes in v5:
time: 163 us; the launch traced here: 162 us
  starting transfers between devices  65.9 us (40%)
  blocking collectives  52.8 us (32%)
  Pallas kernels  18.9 us (12%)
  waiting for transfers between devices  18.4 us (11%)
  other arithmetic  3.37 us (2%)
    all_gather x1, blocking collectives, local(): got = lax.all_gather(payload, Z, axis=0, tiled=False)  35 us
    ppermute x6, starting transfers between devices, turn(): return lax.ppermute(v, 'x', [(i, (i + k) % NX) for i in range(NX)])  23.8 us
    all_to_all x3, starting transfers between devices, exchange(): return lax.all_to_all(v, axes, 0, 0, tiled=True)  21.3 us
    ppermute x4, starting transfers between devices, swap(): return lax.ppermute(v, axis, [(0, 1), (1, 0)])  20.8 us
    pallas_call x5, Pallas kernels, call(): pl.pallas_call(kernel, out_shape=tuple((pltpu.HBM(o.shape, o.dtype) for o...  18.9 us
    all_to_all x1, blocking collectives, exchange(): return lax.all_to_all(v, axes, 0, 0, tiled=True)  17.8 us
    all_to_all x3, waiting for transfers between devices, exchange(): return lax.all_to_all(v, axes, 0, 0, tiled=True)  12.8 us
    ppermute x6, waiting for transfers between devices, turn(): return lax.ppermute(v, 'x', [(i, (i + k) % NX) for i in range(NX)])  5.02 us
  transfers between devices with their start and end apart: 13, of which 5 were waited for; matrix products, arithmetic and copies ran while one was open for 1% of the time, Pallas kernels for 10%

profile of v5, /device:TPU:32, one launch (start us, length us, event | category | flops | bytes accessed | tf_op | source)
XLA Modules:
  0.0 161.8 jit_solution(5788559710024393660)
XLA Ops:
  0.6 1.0 pad_maximum_fusion.refs_3_
  1.6 0.0 copy-start.2
  1.7 14.8 %collective-permute-start = (bf16[3,172,256]{2,1,0:T(8,128)(2,1)S(1)}, bf16[3,172,256]{2,1,0:T(8,128)(2,1)S(1)}, u32[]{:S(2)}, u32[]{:S(2)}) collective-permute-start(bf16[3,172,256]{2,1,0:T(8,128)(2,1)S(1)} %pad_maximum_fusion.refs_3_), channel_id=1, source_target_pairs={{0,256},{256,0},{1,257},{257,1},{2,258},{258,2},{3,259},{259,3},{4... | collective-permute-start | bytes 792584 | tf_op jit(solution)/shard_map/ppermute | solution.py:246
  16.5 3.4 %collective-permute-start.1 = (bf16[3,172,256]{2,1,0:T(8,128)(2,1)S(1)}, bf16[3,172,256]{2,1,0:T(8,128)(2,1)S(1)}, u32[]{:S(2)}, u32[]{:S(2)}) collective-permute-start(bf16[3,172,256]{2,1,0:T(8,128)(2,1)S(1)} %pad_maximum_fusion.refs_3_), channel_id=1, source_target_pairs={{0,64},{64,128},{128,192},{192,0},{1,65},{65,129},{129,193},{193,1... | collective-permute-start | bytes 792584 | tf_op jit(solution)/shard_map/ppermute | solution.py:250
  19.9 4.6 %collective-permute-start.2 = (bf16[3,172,256]{2,1,0:T(8,128)(2,1)S(1)}, bf16[3,172,256]{2,1,0:T(8,128)(2,1)S(1)}, u32[]{:S(2)}, u32[]{:S(2)}) collective-permute-start(bf16[3,172,256]{2,1,0:T(8,128)(2,1)S(1)} %pad_maximum_fusion.refs_3_), channel_id=1, source_target_pairs={{0,128},{64,192},{128,0},{192,64},{1,129},{65,193},{129,1},{193,65... | collective-permute-start | bytes 792584 | tf_op jit(solution)/shard_map/ppermute | solution.py:250
  24.5 3.3 %collective-permute-start.3 = (bf16[3,172,256]{2,1,0:T(8,128)(2,1)S(1)}, bf16[3,172,256]{2,1,0:T(8,128)(2,1)S(1)}, u32[]{:S(2)}, u32[]{:S(2)}) collective-permute-start(bf16[3,172,256]{2,1,0:T(8,128)(2,1)S(1)} %pad_maximum_fusion.refs_3_), channel_id=1, source_target_pairs={{0,192},{64,0},{128,64},{192,128},{1,193},{65,1},{129,65},{193,129... | collective-permute-start | bytes 792584 | tf_op jit(solution)/shard_map/ppermute | solution.py:250
  27.9 1.4 shard_map.129
  29.3 0.1 pad_add_fusion.refs_0_
  29.4 35.0 %all-gather = bf16[1152,128]{1,0:T(8,128)(2,1)S(1)} all-gather(bf16[72,128]{1,0:T(8,128)(2,1)} %shard_map.129), channel_id=2, replica_groups=mesh['zh'=2,'x'=4,'y'=4,'zl'=8,'c'=2] {'zh','zl'}, dimensions={0}, use_global_device_ids=true | all-gather | bytes 313344 | tf_op jit(solution)/shard_map/all_gather | solution.py:281
  64.4 0.0 collective-permute-done.refs_7_
  64.4 0.0 copy-start.4
  64.4 2.3 %shard_map.130 = (bf16[16,96,256]{2,1,0:T(8,128)(2,1)}, bf16[16,96,256]{2,1,0:T(8,128)(2,1)}, bf16[2,128,192]{2,1,0:T(8,128)(2,1)}, f32[2,192,128]{2,1,0:T(8,128)}) custom-call(s32[3]{0:T(128)S(1)} %pad_add_fusion.refs_0_, bf16[16,72,128]{2,1,0:T(8,128)(2,1)S(1)} %bitcast.26), custom_call_target="tpu_custom_call" | custom-call | tf_op jit(solution)/shard_map/pallas_call | solution.py:53
  66.8 0.0 collective-permute-done.1.refs_4_
  66.8 0.0 copy-start.5
  66.8 0.0 collective-permute-done.2.refs_5_
  66.8 0.0 copy-start.6
  66.8 0.0 collective-permute-done.3.refs_6_
  66.8 0.0 copy-start.7
  66.8 0.8 copy-done.7
  67.6 7.0 %all-to-all-start = ((bf16[16,96,256]{2,1,0:T(8,128)(2,1)}), bf16[16,96,256]{2,1,0:T(8,128)(2,1)S(1)}, u32[]{:S(2)}, u32[]{:S(2)}) async-start(bf16[16,96,256]{2,1,0:T(8,128)(2,1)} %get-tuple-element.35), calls=%async_computation | async-start | bytes 1572864 | tf_op jit(solution)/shard_map/all_to_all | solution.py:254
  74.6 5.3 %collective-permute-start.4 = (bf16[3,172,256]{2,1,0:T(8,128)(2,1)S(1)}, bf16[3,172,256]{2,1,0:T(8,128)(2,1)S(1)}, u32[]{:S(2)}, u32[]{:S(2)}) collective-permute-start(bf16[3,172,256]{2,1,0:T(8,128)(2,1)S(1)} %collective-permute-done.refs_7_), channel_id=1, source_target_pairs={{0,128},{64,192},{128,0},{192,64},{1,129},{65,193},{129,1},{193,65... | collective-permute-start | bytes 792584 | tf_op jit(solution)/shard_map/ppermute | solution.py:250
  80.0 2.5 %collective-permute-start.5 = (bf16[3,172,256]{2,1,0:T(8,128)(2,1)S(1)}, bf16[3,172,256]{2,1,0:T(8,128)(2,1)S(1)}, u32[]{:S(2)}, u32[]{:S(2)}) collective-permute-start(bf16[3,172,256]{2,1,0:T(8,128)(2,1)S(1)} %collective-permute-done.refs_7_), channel_id=1, source_target_pairs={{0,64},{64,128},{128,192},{192,0},{1,65},{65,129},{129,193},{193,1... | collective-permute-start | bytes 792584 | tf_op jit(solution)/shard_map/ppermute | solution.py:250
  82.4 4.6 %collective-permute-start.6 = (bf16[3,172,256]{2,1,0:T(8,128)(2,1)S(1)}, bf16[3,172,256]{2,1,0:T(8,128)(2,1)S(1)}, u32[]{:S(2)}, u32[]{:S(2)}) collective-permute-start(bf16[3,172,256]{2,1,0:T(8,128)(2,1)S(1)} %collective-permute-done.refs_7_), channel_id=1, source_target_pairs={{0,192},{64,0},{128,64},{192,128},{1,193},{65,1},{129,65},{193,129... | collective-permute-start | bytes 792584 | tf_op jit(solution)/shard_map/ppermute | solution.py:250
  87.0 2.2 %collective-permute-done.4.refs_9_ = bf16[3,172,256]{2,1,0:T(8,128)(2,1)S(1)} collective-permute-done((bf16[3,172,256]{2,1,0:T(8,128)(2,1)S(1)}, bf16[3,172,256]{2,1,0:T(8,128)(2,1)S(1)}, u32[]{:S(2)}, u32[]{:S(2)}) %collective-permute-start.4) | collective-permute-done | bytes 264224 | tf_op jit(solution)/shard_map/ppermute | solution.py:250
  89.2 0.0 copy-start.8
  89.3 2.8 %collective-permute-done.5.refs_8_ = bf16[3,172,256]{2,1,0:T(8,128)(2,1)S(1)} collective-permute-done((bf16[3,172,256]{2,1,0:T(8,128)(2,1)S(1)}, bf16[3,172,256]{2,1,0:T(8,128)(2,1)S(1)}, u32[]{:S(2)}, u32[]{:S(2)}) %collective-permute-start.5) | collective-permute-done | bytes 264224 | tf_op jit(solution)/shard_map/ppermute | solution.py:250
  92.0 0.0 copy-start.9
  92.0 0.0 collective-permute-done.6.refs_10_
  92.0 0.0 copy-start.10
  92.0 0.7 copy-done.10
  92.8 0.0 all-to-all-done.refs_1_
  92.8 0.0 copy-start
  92.8 1.9 %collective-permute-start.8 = (bf16[16,96,256]{2,1,0:T(8,128)(2,1)S(1)}, bf16[16,96,256]{2,1,0:T(8,128)(2,1)S(1)}, u32[]{:S(2)}, u32[]{:S(2)}) collective-permute-start(bf16[16,96,256]{2,1,0:T(8,128)(2,1)S(1)} %all-to-all-done.refs_1_), channel_id=1, source_target_pairs={{0,1},{1,0},{2,3},{3,2},{4,5},{5,4},{6,7},{7,6},{8,9},{9,8},{10,11... | collective-permute-start | bytes 2359304 | tf_op jit(solution)/shard_map/ppermute | solution.py:246
  94.7 0.0 copy-done.8
  94.7 0.0 copy-done.9
  94.7 0.0 copy-done.2
  94.7 0.0 copy-done.4
  94.7 0.0 copy-done.5
  94.8 0.0 copy-done.6
  94.8 6.4 %all-to-all-start.1 = ((bf16[16,96,256]{2,1,0:T(8,128)(2,1)}), bf16[16,96,256]{2,1,0:T(8,128)(2,1)S(1)}, u32[]{:S(2)}, u32[]{:S(2)}) async-start(bf16[16,96,256]{2,1,0:T(8,128)(2,1)} %get-tuple-element.38), calls=%async_computation.1 | async-start | bytes 1572864 | tf_op jit(solution)/shard_map/all_to_all | solution.py:254
  101.2 0.0 collective-permute-done.8.refs_2_
  101.2 0.0 copy-done
  101.2 7.1 %shard_map.131 = (f32[16,96,256]{2,1,0:T(8,128)}, bf16[16,96,256]{2,1,0:T(8,128)(2,1)}, bf16[384,2048]{1,0:T(8,128)(2,1)}, f32[416,384]{1,0:T(8,128)}, bf16[208,...) custom-call(s32[3]{0:T(128)S(1)} %pad_add_fusion.refs_0_, bf16[16,96,256]{2,1,0:T(8,128)(2,1)} %copy-done, ...), custom_call_target="tpu_custom_call" | custom-call | tf_op jit(solution)/shard_map/pallas_call | solution.py:53
  108.3 2.1 %collective-permute-start.9 = (bf16[16,96,256]{2,1,0:T(8,128)(2,1)}, bf16[16,96,256]{2,1,0:T(8,128)(2,1)S(1)}, u32[]{:S(2)}, u32[]{:S(2)}) collective-permute-start(bf16[16,96,256]{2,1,0:T(8,128)(2,1)} %get-tuple-element.47), channel_id=1, source_target_pairs={{0,1},{1,0},{2,3},{3,2},{4,5},{5,4},{6,7},{7,6},{8,9},{9,8},{10,11... | collective-permute-start | bytes 2359304 | tf_op jit(solution)/shard_map/ppermute | solution.py:246
  110.4 6.1 %all-to-all-done.1.refs_1_ = bf16[16,96,256]{2,1,0:T(8,128)(2,1)S(1)} async-done(((bf16[16,96,256]{2,1,0:T(8,128)(2,1)}), bf16[16,96,256]{2,1,0:T(8,128)(2,1)S(1)}, u32[]{:S(2)}, u32[]{:S(2)}) %all-to-all-start.1) | async-done | bytes 786464 | tf_op jit(solution)/shard_map/all_to_all | solution.py:254
  116.4 0.0 copy-start.1
  116.4 1.9 %collective-permute-start.7 = (bf16[16,96,256]{2,1,0:T(8,128)(2,1)S(1)}, bf16[16,96,256]{2,1,0:T(8,128)(2,1)S(1)}, u32[]{:S(2)}, u32[]{:S(2)}) collective-permute-start(bf16[16,96,256]{2,1,0:T(8,128)(2,1)S(1)} %all-to-all-done.1.refs_1_), channel_id=1, source_target_pairs={{0,1},{1,0},{2,3},{3,2},{4,5},{5,4},{6,7},{7,6},{8,9},{9,8},{10,11... | collective-permute-start | bytes 2359304 | tf_op jit(solution)/shard_map/ppermute | solution.py:246
  118.4 0.0 collective-permute-done.9
  118.4 1.7 %add_convert_fusion = bf16[16,96,256]{2,1,0:T(8,128)(2,1)S(1)} fusion(f32[16,96,256]{2,1,0:T(8,128)} %get-tuple-element.46, bf16[16,96,256]{2,1,0:T(8,128)(2,1)S(1)} %collective-permute-done.9), kind=kLoop, calls=%fused_computation | loop fusion | flops 1179648 | bytes 3145728 | tf_op jit(solution)/shard_map/convert_element_type | solution.py:323
  120.0 0.0 copy-done.1
  120.0 0.6 collective-permute-done.7.refs_2_
  120.6 0.0 copy-start.3
  120.6 17.8 %all_to_all.20.refs_0_ = bf16[16,96,256]{2,1,0:T(8,128)(2,1)S(1)} all-to-all(bf16[16,96,256]{2,1,0:T(8,128)(2,1)S(1)} %add_convert_fusion), channel_id=1, replica_groups=mesh['zh'=2,'x'=4,'y'=4,'zl'=8,'c'=2] {'x','y'}, dimensions={0} | all-to-all | bytes 1572864 | tf_op jit(solution)/shard_map/all_to_all | solution.py:254
  138.4 2.1 %shard_map.132 = bf16[16,32,128]{2,1,0:T(8,128)(2,1)} custom-call(bf16[16,96,256]{2,1,0:T(8,128)(2,1)S(1)} %all_to_all.20.refs_0_, bf16[2,128,192]{2,1,0:T(8,128)(2,1)} %get-tuple-element.49.refs_1_, f32[2,192,128]{2,1,0:T(8,128)} %get-tuple-element.50.refs_2_), custom_call_target="tpu_custom_call" | custom-call | tf_op jit(solution)/shard_map/pallas_call | solution.py:53
  140.5 7.9 %all-to-all-start.3 = ((bf16[16,32,128]{2,1,0:T(8,128)(2,1)}), bf16[16,32,128]{2,1,0:T(8,128)(2,1)S(1)}, u32[]{:S(2)}, u32[]{:S(2)}) async-start(bf16[16,32,128]{2,1,0:T(8,128)(2,1)} %shard_map.132), calls=%async_computation.3 | async-start | bytes 262144 | tf_op jit(solution)/shard_map/all_to_all | solution.py:254
  148.4 0.0 copy-done.3
  148.4 6.0 %shard_map.133 = (bf16[192,2048]{1,0:T(8,128)(2,1)}, bf16[192,2048]{1,0:T(8,128)(2,1)}, bf16[192,2048]{1,0:T(8,128)(2,1)}) custom-call(s32[3]{0:T(128)S(1)} %pad_add_fusion.refs_0_, bf16[16,96,256]{2,1,0:T(8,128)(2,1)} %copy-done.1, bf16[16,96,256]{2,1,0:T(8,128)(2,1)} %copy-done.3, bf16[384,2048]{1,0:T(8,128)(2,1)} %get-tuple-element.53.refs_3_, ...), custom_call_target="tpu_custom_call" | custom-call | tf_op jit(solution)/shard_map/pallas_call | solution.py:53
  154.4 6.7 %all-to-all-done.3 = bf16[16,32,128]{2,1,0:T(8,128)(2,1)S(1)} async-done(((bf16[16,32,128]{2,1,0:T(8,128)(2,1)}), bf16[16,32,128]{2,1,0:T(8,128)(2,1)S(1)}, u32[]{:S(2)}, u32[]{:S(2)}) %all-to-all-start.3) | async-done | bytes 131104 | tf_op jit(solution)/shard_map/all_to_all | solution.py:254
  161.2 0.6 reduce_sum.12
Async XLA Ops:
  1.6 93.1 %copy-start.2 = (bf16[3,172,256]{2,1,0:T(8,128)(2,1)}, bf16[3,172,256]{2,1,0:T(8,128)(2,1)S(1)}, u32[]{:S(2)}) copy-start(bf16[3,172,256]{2,1,0:T(8,128)(2,1)S(1)} %pad_maximum_fusion.refs_3_) | copy-start | bytes 792580
  1.7 62.8 %collective-permute-start = (bf16[3,172,256]{2,1,0:T(8,128)(2,1)S(1)}, bf16[3,172,256]{2,1,0:T(8,128)(2,1)S(1)}, u32[]{:S(2)}, u32[]{:S(2)}) collective-permute-start(bf16[3,172,256]{2,1,0:T(8,128)(2,1)S(1)} %pad_maximum_fusion.refs_3_), channel_id=1, source_target_pairs={{0,256},{256,0},{1,257},{257,1},{2,258},{258,2},{3,259},{259,3},{4... | collective-permute-start | bytes 792584 | tf_op jit(solution)/shard_map/ppermute | solution.py:246
  16.5 50.3 %collective-permute-start.1 = (bf16[3,172,256]{2,1,0:T(8,128)(2,1)S(1)}, bf16[3,172,256]{2,1,0:T(8,128)(2,1)S(1)}, u32[]{:S(2)}, u32[]{:S(2)}) collective-permute-start(bf16[3,172,256]{2,1,0:T(8,128)(2,1)S(1)} %pad_maximum_fusion.refs_3_), channel_id=1, source_target_pairs={{0,64},{64,128},{128,192},{192,0},{1,65},{65,129},{129,193},{193,1... | collective-permute-start | bytes 792584 | tf_op jit(solution)/shard_map/ppermute | solution.py:250
  19.9 46.9 %collective-permute-start.2 = (bf16[3,172,256]{2,1,0:T(8,128)(2,1)S(1)}, bf16[3,172,256]{2,1,0:T(8,128)(2,1)S(1)}, u32[]{:S(2)}, u32[]{:S(2)}) collective-permute-start(bf16[3,172,256]{2,1,0:T(8,128)(2,1)S(1)} %pad_maximum_fusion.refs_3_), channel_id=1, source_target_pairs={{0,128},{64,192},{128,0},{192,64},{1,129},{65,193},{129,1},{193,65... | collective-permute-start | bytes 792584 | tf_op jit(solution)/shard_map/ppermute | solution.py:250
  24.5 42.3 %collective-permute-start.3 = (bf16[3,172,256]{2,1,0:T(8,128)(2,1)S(1)}, bf16[3,172,256]{2,1,0:T(8,128)(2,1)S(1)}, u32[]{:S(2)}, u32[]{:S(2)}) collective-permute-start(bf16[3,172,256]{2,1,0:T(8,128)(2,1)S(1)} %pad_maximum_fusion.refs_3_), channel_id=1, source_target_pairs={{0,192},{64,0},{128,64},{192,128},{1,193},{65,1},{129,65},{193,129... | collective-permute-start | bytes 792584 | tf_op jit(solution)/shard_map/ppermute | solution.py:250
  64.4 30.3 %copy-start.4 = (bf16[3,172,256]{2,1,0:T(8,128)(2,1)}, bf16[3,172,256]{2,1,0:T(8,128)(2,1)S(1)}, u32[]{:S(2)}) copy-start(bf16[3,172,256]{2,1,0:T(8,128)(2,1)S(1)} %collective-permute-done.refs_7_) | copy-start | bytes 792580
  66.8 28.0 %copy-start.5 = (bf16[3,172,256]{2,1,0:T(8,128)(2,1)}, bf16[3,172,256]{2,1,0:T(8,128)(2,1)S(1)}, u32[]{:S(2)}) copy-start(bf16[3,172,256]{2,1,0:T(8,128)(2,1)S(1)} %collective-permute-done.1.refs_4_) | copy-start | bytes 792580
  66.8 28.0 %copy-start.6 = (bf16[3,172,256]{2,1,0:T(8,128)(2,1)}, bf16[3,172,256]{2,1,0:T(8,128)(2,1)S(1)}, u32[]{:S(2)}) copy-start(bf16[3,172,256]{2,1,0:T(8,128)(2,1)S(1)} %collective-permute-done.2.refs_5_) | copy-start | bytes 792580
  66.8 0.8 copy-start.7
  67.6 25.2 %all-to-all-start = ((bf16[16,96,256]{2,1,0:T(8,128)(2,1)}), bf16[16,96,256]{2,1,0:T(8,128)(2,1)S(1)}, u32[]{:S(2)}, u32[]{:S(2)}) async-start(bf16[16,96,256]{2,1,0:T(8,128)(2,1)} %get-tuple-element.35), calls=%async_computation | async-start | bytes 1572864 | tf_op jit(solution)/shard_map/all_to_all | solution.py:254
  74.6 14.6 %collective-permute-start.4 = (bf16[3,172,256]{2,1,0:T(8,128)(2,1)S(1)}, bf16[3,172,256]{2,1,0:T(8,128)(2,1)S(1)}, u32[]{:S(2)}, u32[]{:S(2)}) collective-permute-start(bf16[3,172,256]{2,1,0:T(8,128)(2,1)S(1)} %collective-permute-done.refs_7_), channel_id=1, source_target_pairs={{0,128},{64,192},{128,0},{192,64},{1,129},{65,193},{129,1},{193,65... | collective-permute-start | bytes 792584 | tf_op jit(solution)/shard_map/ppermute | solution.py:250
  80.0 12.1 %collective-permute-start.5 = (bf16[3,172,256]{2,1,0:T(8,128)(2,1)S(1)}, bf16[3,172,256]{2,1,0:T(8,128)(2,1)S(1)}, u32[]{:S(2)}, u32[]{:S(2)}) collective-permute-start(bf16[3,172,256]{2,1,0:T(8,128)(2,1)S(1)} %collective-permute-done.refs_7_), channel_id=1, source_target_pairs={{0,64},{64,128},{128,192},{192,0},{1,65},{65,129},{129,193},{193,1... | collective-permute-start | bytes 792584 | tf_op jit(solution)/shard_map/ppermute | solution.py:250
  82.4 9.6 %collective-permute-start.6 = (bf16[3,172,256]{2,1,0:T(8,128)(2,1)S(1)}, bf16[3,172,256]{2,1,0:T(8,128)(2,1)S(1)}, u32[]{:S(2)}, u32[]{:S(2)}) collective-permute-start(bf16[3,172,256]{2,1,0:T(8,128)(2,1)S(1)} %collective-permute-done.refs_7_), channel_id=1, source_target_pairs={{0,192},{64,0},{128,64},{192,128},{1,193},{65,1},{129,65},{193,129... | collective-permute-start | bytes 792584 | tf_op jit(solution)/shard_map/ppermute | solution.py:250
  89.2 5.5 %copy-start.8 = (bf16[3,172,256]{2,1,0:T(8,128)(2,1)}, bf16[3,172,256]{2,1,0:T(8,128)(2,1)S(1)}, u32[]{:S(2)}) copy-start(bf16[3,172,256]{2,1,0:T(8,128)(2,1)S(1)} %collective-permute-done.4.refs_9_) | copy-start | bytes 792580
  92.0 2.7 %copy-start.9 = (bf16[3,172,256]{2,1,0:T(8,128)(2,1)}, bf16[3,172,256]{2,1,0:T(8,128)(2,1)S(1)}, u32[]{:S(2)}) copy-start(bf16[3,172,256]{2,1,0:T(8,128)(2,1)S(1)} %collective-permute-done.5.refs_8_) | copy-start | bytes 792580
  92.0 0.7 copy-start.10
  92.8 8.4 %copy-start = (bf16[16,96,256]{2,1,0:T(8,128)(2,1)}, bf16[16,96,256]{2,1,0:T(8,128)(2,1)S(1)}, u32[]{:S(2)}) copy-start(bf16[16,96,256]{2,1,0:T(8,128)(2,1)S(1)} %all-to-all-done.refs_1_) | copy-start | bytes 2359300
  92.8 8.4 %collective-permute-start.8 = (bf16[16,96,256]{2,1,0:T(8,128)(2,1)S(1)}, bf16[16,96,256]{2,1,0:T(8,128)(2,1)S(1)}, u32[]{:S(2)}, u32[]{:S(2)}) collective-permute-start(bf16[16,96,256]{2,1,0:T(8,128)(2,1)S(1)} %all-to-all-done.refs_1_), channel_id=1, source_target_pairs={{0,1},{1,0},{2,3},{3,2},{4,5},{5,4},{6,7},{7,6},{8,9},{9,8},{10,11... | collective-permute-start | bytes 2359304 | tf_op jit(solution)/shard_map/ppermute | solution.py:246
  94.8 21.7 %all-to-all-start.1 = ((bf16[16,96,256]{2,1,0:T(8,128)(2,1)}), bf16[16,96,256]{2,1,0:T(8,128)(2,1)S(1)}, u32[]{:S(2)}, u32[]{:S(2)}) async-start(bf16[16,96,256]{2,1,0:T(8,128)(2,1)} %get-tuple-element.38), calls=%async_computation.1 | async-start | bytes 1572864 | tf_op jit(solution)/shard_map/all_to_all | solution.py:254
  108.3 10.1 %collective-permute-start.9 = (bf16[16,96,256]{2,1,0:T(8,128)(2,1)}, bf16[16,96,256]{2,1,0:T(8,128)(2,1)S(1)}, u32[]{:S(2)}, u32[]{:S(2)}) collective-permute-start(bf16[16,96,256]{2,1,0:T(8,128)(2,1)} %get-tuple-element.47), channel_id=1, source_target_pairs={{0,1},{1,0},{2,3},{3,2},{4,5},{5,4},{6,7},{7,6},{8,9},{9,8},{10,11... | collective-permute-start | bytes 2359304 | tf_op jit(solution)/shard_map/ppermute | solution.py:246
  116.4 3.6 %copy-start.1 = (bf16[16,96,256]{2,1,0:T(8,128)(2,1)}, bf16[16,96,256]{2,1,0:T(8,128)(2,1)S(1)}, u32[]{:S(2)}) copy-start(bf16[16,96,256]{2,1,0:T(8,128)(2,1)S(1)} %all-to-all-done.1.refs_1_) | copy-start | bytes 2359300
  116.4 4.2 %collective-permute-start.7 = (bf16[16,96,256]{2,1,0:T(8,128)(2,1)S(1)}, bf16[16,96,256]{2,1,0:T(8,128)(2,1)S(1)}, u32[]{:S(2)}, u32[]{:S(2)}) collective-permute-start(bf16[16,96,256]{2,1,0:T(8,128)(2,1)S(1)} %all-to-all-done.1.refs_1_), channel_id=1, source_target_pairs={{0,1},{1,0},{2,3},{3,2},{4,5},{5,4},{6,7},{7,6},{8,9},{9,8},{10,11... | collective-permute-start | bytes 2359304 | tf_op jit(solution)/shard_map/ppermute | solution.py:246
  120.6 27.8 %copy-start.3 = (bf16[16,96,256]{2,1,0:T(8,128)(2,1)}, bf16[16,96,256]{2,1,0:T(8,128)(2,1)S(1)}, u32[]{:S(2)}) copy-start(bf16[16,96,256]{2,1,0:T(8,128)(2,1)S(1)} %collective-permute-done.7.refs_2_) | copy-start | bytes 2359300
  140.5 20.7 %all-to-all-start.3 = ((bf16[16,32,128]{2,1,0:T(8,128)(2,1)}), bf16[16,32,128]{2,1,0:T(8,128)(2,1)S(1)}, u32[]{:S(2)}, u32[]{:S(2)}) async-start(bf16[16,32,128]{2,1,0:T(8,128)(2,1)} %shard_map.132), calls=%async_computation.3 | async-start | bytes 262144 | tf_op jit(solution)/shard_map/all_to_all | solution.py:254
